TPU v7x, 32 devices: a whole 2x2x4 slice. The times are simulated.
32 devices in a mesh: ens: 2 (over y), lon: 4 (over z), dom: 4 (over x, core).
Axes of the slice: x: 2, y: 2, z: 4, core: 2. Of those that a mesh axis runs over, the one named last changes fastest.
Arguments:
- particles: bfloat16 [16, 69, 96, 256], P(('ens', 'dom'), None, 'lon'), parts along dimension 0, may hold values from -6 to 6
- observed: bfloat16 [138, 96, 256], P('ens', 'lon'), parts along dimension 0, may hold values from -6 to 6
- precision: float32 [192, 256], P(('ens', 'lon')), parts along dimension 0, may hold values from 0.25 to 12, as said below
- stations: int32 [192, 256], P(('ens', 'lon')), parts along dimension 0, may hold values 0 or 1
- ancestors: int32 [16], P(('ens', 'dom')), parts along dimension 0, may hold values from 0 to 7
- tempering: float32 [2], P('ens'), parts along dimension 0, may hold values from 1 to 4
- w_in: bfloat16 [3, 3, 64, 69], replicated, may hold values from -0.25 to 0.25
- w_mid: bfloat16 [3, 3, 64, 64], replicated, may hold values from -0.25 to 0.25
- w_out: bfloat16 [3, 3, 69, 64], replicated, may hold values from -0.25 to 0.25
Outputs:
- new_particles: bfloat16 [16, 69, 96, 256], P(('ens', 'dom'), None, 'lon'), parts along dimension 0
- weights: float32 [16], P(('ens', 'dom')), parts along dimension 0
There are 2 independent parts, one for each index of `ens`. A program takes and returns all parts, laid end to end along the dimension named above; an argument that names none is the same for every part. Nothing has to cross between parts.
Inputs may be any that keep to these rules, and one draw needn't show every extreme that they name: `precision`: positive everywhere; no other structure is promised. Slot s continues particle ancestors[s]; a particle may be continued by several slots or by none.
All inputs are finite; a program needn't handle non-finite values. No bound on the sum of `stations` on one device may be relied on, other than what follows from the above.
Results may differ from a plain program's by a relative error of at most 0.0021.
Values may be sent and summed in bfloat16 or wider, within the bound.
A program may use at most 128 MiB of HBM per device.

v0:
```python
import jax
import jax.numpy as jnp
from jax import lax
from jax.sharding import PartitionSpec as P


def extended_2(block, sides, width):
    for axis, dim in sides:
        count = lax.axis_size(axis)
        forward = [(i, i + 1) for i in range(count - 1)]
        forward.append((count - 1, 0))
        backward = [(target, source) for source, target in forward]
        low = lax.ppermute(
            lax.slice_in_dim(block, block.shape[dim] - width, None, axis=dim), axis, forward
        )
        high = lax.ppermute(lax.slice_in_dim(block, 0, width, axis=dim), axis, backward)
        block = jnp.concatenate([low, block, high], axis=dim)
    return block


def conv_local(extended, weight):
    out_width = extended.shape[2] - 2
    lat_rows = extended.shape[3]
    padded = jnp.pad(extended, ((0, 0), (0, 0), (0, 0), (1, 1)))
    summed = jnp.zeros((extended.shape[0], weight.shape[2], out_width, lat_rows), jnp.float32)
    for row_tap in range(3):
        for col_tap in range(3):
            window = padded[:, :, row_tap : row_tap + out_width, col_tap : col_tap + lat_rows]
            summed = summed + jnp.einsum(
                "oc,pcxy->poxy",
                weight[row_tap, col_tap],
                window,
                preferred_element_type=jnp.float32,
            )
    return summed


def denoise_local(states, observed, obs_weight, w_in, w_mid, w_out):
    extended = extended_2(states, (("lon", 2),), 1)
    first_act = jax.nn.silu(conv_local(extended, w_in)).astype(jnp.bfloat16)
    first_ext = extended_2(first_act, (("lon", 2),), 1)
    second_act = jax.nn.silu(conv_local(first_ext, w_mid)).astype(jnp.bfloat16)
    second_ext = extended_2(second_act, (("lon", 2),), 1)
    noise_pred = conv_local(second_ext, w_out)
    current = states.astype(jnp.float32)
    updated = (
        current
        - 0.5 * noise_pred
        + 0.25 * obs_weight[None, None] * (observed.astype(jnp.float32)[None] - current)
    )
    return updated.astype(jnp.bfloat16)


def continue_slots(slabs, slot_ancestors):
    slab_piece = lax.all_gather(slabs, "dom", axis=0, tiled=True)
    piece_rows = slab_piece.shape[0]
    inside = (slot_ancestors >= 0) & (slot_ancestors < piece_rows)
    chosen = jnp.take(slab_piece, jnp.clip(slot_ancestors, 0, piece_rows - 1), axis=0)
    return jnp.where(inside[:, None, None, None], chosen, jnp.zeros_like(slabs))


def on_device(particles, observed, precision, stations, ancestors, tempering, w_in, w_mid, w_out):
    obs_weight = stations.astype(jnp.float32) * precision
    misfit_cell = particles.astype(jnp.float32) - observed.astype(jnp.float32)[None]
    local_sums = jnp.sum(obs_weight[None, None] * misfit_cell * misfit_cell, axis=(1, 2, 3))
    band_sums = lax.psum(local_sums, "lon")
    every_sum = lax.all_gather(band_sums, "dom", axis=0, tiled=True)
    center = jnp.mean(every_sum)
    deviation = every_sum - center
    spread = jnp.sqrt(jnp.mean(deviation * deviation) + 1.0)
    log_weights = -0.5 * tempering[0] * deviation / spread
    expo = jnp.exp(log_weights)
    weights_all = expo / jnp.sum(expo)
    slot_count = ancestors.shape[0]
    own_weights = lax.dynamic_slice_in_dim(
        weights_all, lax.axis_index("dom") * slot_count, slot_count
    )
    continued = continue_slots(particles, ancestors)
    new_particles = denoise_local(continued, observed, obs_weight, w_in, w_mid, w_out)
    return (new_particles, own_weights)


def solution(mesh):
    return jax.shard_map(
        on_device,
        mesh=mesh,
        in_specs=(
            P(("ens", "dom"), None, "lon", None),
            P("ens", "lon", None),
            P(("ens", "lon"), None),
            P(("ens", "lon"), None),
            P(("ens", "dom")),
            P("ens"),
            P(),
            P(),
            P(),
        ),
        out_specs=(P(("ens", "dom"), None, "lon", None), P(("ens", "dom"))),
        check_vma=False,
    )
```

profile of v0, /device:TPU:0, one launch (start us, length us, event | category | flops | bytes accessed | tf_op | source)
XLA Modules:
  0.0 159.0 jit_solution(17750243368687318687)
XLA Ops:
  10.2 13.4 %psum.7 = f32[2]{0:T(128)S(1)} all-reduce(f32[2]{0:T(128)S(1)} %fusion.5), channel_id=1, replica_groups=mesh['ens'=2,'lon'=4,'dom'=4] {'lon'}, use_global_device_ids=true, to_apply=%region_1.0 | all-reduce | flops 2 | bytes 16 | tf_op jit(solution)/shard_map/psum | solution.py:66
  25.1 6.1 %all-reduce.3 = f32[8]{0:T(128)S(1)} all-reduce(f32[8]{0:T(128)S(1)} %dynamic-update-slice), channel_id=1, replica_groups=mesh['ens'=2,'lon'=4,'dom'=4] {'dom'}, use_global_device_ids=true, to_apply=%add.3 | all-reduce | flops 8 | bytes 64
  36.4 25.2 %all-gather.2.cloned.1.call-done = bf16[8,69,24,256]{3,2,1,0:T(8,128)(2,1)} async-done(((bf16[2,69,24,256]{3,2,1,0:T(8,128)(2,1)}), bf16[8,69,24,256]{3,2,1,0:T(8,128)(2,1)}) %all-gather.2.cloned.1.call-update) | async-done | bytes 6782992 | tf_op jit(solution)/shard_map/all_gather | solution.py:55
  61.6 3.6 %gather_fusion = bf16[2,69,24,256]{3,2,1,0:T(8,128)(2,1)S(1)} fusion(bf16[8,69,24,256]{3,2,1,0:T(8,128)(2,1)} %all-gather.2.cloned.1.call-done, s32[1024]{0:T(1024)S(1)} %pad_clamp_fusion), kind=kCustom, calls=%fused_computation | custom fusion | bytes 3391496 | tf_op jit(solution)/shard_map/jit(_take)/gather | solution.py:58
  67.2 2.3 %collective-permute-start.1 = (bf16[2,69,1,256]{3,1,2,0:T(8,128)(2,1)S(1)}, bf16[2,69,1,256]{3,1,2,0:T(8,128)(2,1)S(1)}, u32[]{:S(2)}, u32[]{:S(2)}) collective-permute-start(bf16[2,69,1,256]{3,1,2,0:T(8,128)(2,1)S(1)} %get-tuple-element.15), channel_id=1, source_target_pairs={{4,0},{8,4},{12,8},{0,12},{5,1},{9,5},{13,9},{1,13},{6,2},{10,6},{... | collective-permute-start | bytes 211976 | tf_op jit(solution)/shard_map/ppermute | solution.py:16
  69.6 2.6 %fusion.111 = f32[2,24,256,64]{2,3,1,0:T(8,128)} fusion(bf16[3,3,64,69]{3,2,1,0:T(8,128)(2,1)S(1)} %copy-done.3, bf16[2,69,24,256]{3,2,1,0:T(8,128)(2,1)S(1)} %gather_fusion, pred[2]{0:T(512)(128)(4,1)S(1)} %get-tuple-element.12, pred[2]{0:T(512)(128)(4,1)S(1)} %get-tuple-element.20), kind=kOutput, calls=%fused_computation.123 | convolution fusion | flops 110223360 | bytes 4858880 | tf_op jit(solution)/shard_map/oc,pcxy->poxy/dot_general | solution.py:29
  77.8 2.2 %fusion.42 = f32[2,24,256,64]{2,3,1,0:T(8,128)} fusion(bf16[2,69,26,258]{3,1,2,0:T(8,128)(2,1)S(1)} %fusion.18, bf16[3,3,64,69]{3,2,1,0:T(8,128)(2,1)S(1)} %copy-done.3), kind=kOutput, calls=%fused_computation.56 | convolution fusion | flops 108527616 | bytes 4931584 | tf_op jit(solution)/shard_map/oc,pcxy->poxy/dot_general | solution.py:29
  80.0 2.2 %fusion.24 = f32[2,24,256,64]{2,3,1,0:T(8,128)} fusion(bf16[2,69,24,256]{3,1,2,0:T(8,128)(2,1)S(1)} %fusion.44, bf16[2,69,1,256]{3,1,2,0:T(8,128)(2,1)S(1)} %collective-permute-done, bf16[3,3,64,69]{3,2,1,0:T(8,128)(2,1)S(1)} %copy-done.3), kind=kOutput, calls=%fused_computation.38 | convolution fusion | flops 112060416 | bytes 5005312 | tf_op jit(solution)/shard_map/oc,pcxy->poxy/dot_general | solution.py:29
  82.2 2.2 %fusion.28 = f32[2,24,256,64]{2,3,1,0:T(8,128)} fusion(bf16[2,69,1,256]{3,1,2,0:T(8,128)(2,1)S(1)} %collective-permute-done.1, bf16[2,69,24,256]{3,1,2,0:T(8,128)(2,1)S(1)} %fusion.44, bf16[3,3,64,69]{3,2,1,0:T(8,128)(2,1)S(1)} %copy-done.3), kind=kOutput, calls=%fused_computation.42 | convolution fusion | flops 112060416 | bytes 5005312 | tf_op jit(solution)/shard_map/oc,pcxy->poxy/dot_general | solution.py:29
  84.4 6.0 %fusion.15 = bf16[2,64,24,256]{3,1,2,0:T(8,128)(2,1)S(1)} fusion(f32[2,24,256,64]{2,3,1,0:T(8,128)} %fusion.28, f32[2,24,256,64]{2,3,1,0:T(8,128)S(1)} %fusion.34, f32[2,24,256,64]{2,3,1,0:T(8,128)S(1)} %fusion.36, f32[2,24,256,64]{2,3,1,0:T(8,128)} %fusion.111, f32[2,24,256,64]{2,3,1,0:T(8,128)S(1)} %fusion.38, f32[2,24,256,64]{2,3,1,0:T(8,128)S(1)} %fusion.40, ...), kind=kOutput, calls=%fused_computation.27 | convolution fusion | flops 118751232 | bytes 28524544 | tf_op jit(solution)/shard_map/oc,pcxy->poxy/dot_general | solution.py:29
  91.6 2.7 %collective-permute-start.3 = (bf16[2,64,1,256]{3,1,2,0:T(8,128)(2,1)S(1)}, bf16[2,64,1,256]{3,1,2,0:T(8,128)(2,1)S(1)}, u32[]{:S(2)}, u32[]{:S(2)}) collective-permute-start(bf16[2,64,1,256]{3,1,2,0:T(8,128)(2,1)S(1)} %get-tuple-element.19), channel_id=1, source_target_pairs={{4,0},{8,4},{12,8},{0,12},{5,1},{9,5},{13,9},{1,13},{6,2},{10,6},{... | collective-permute-start | bytes 196616 | tf_op jit(solution)/shard_map/ppermute | solution.py:16
  100.4 2.3 %fusion.81 = f32[2,24,256,64]{2,3,1,0:T(8,128)} fusion(bf16[2,64,26,258]{3,1,2,0:T(8,128)(2,1)S(1)} %fusion.23, bf16[3,3,64,64]{3,2,1,0:T(8,128)(2,1)S(1)} %copy-done.1), kind=kOutput, calls=%fused_computation.91 | convolution fusion | flops 100663296 | bytes 4734976 | tf_op jit(solution)/shard_map/oc,pcxy->poxy/dot_general | solution.py:29
  102.7 2.2 %fusion.85 = f32[2,24,256,64]{2,3,1,0:T(8,128)} fusion(bf16[2,64,26,258]{3,1,2,0:T(8,128)(2,1)S(1)} %fusion.23, bf16[3,3,64,64]{3,2,1,0:T(8,128)(2,1)S(1)} %copy-done.1), kind=kOutput, calls=%fused_computation.96 | convolution fusion | flops 100663296 | bytes 4734976 | tf_op jit(solution)/shard_map/oc,pcxy->poxy/dot_general | solution.py:29
  107.1 2.2 %fusion.73 = f32[2,24,256,64]{2,3,1,0:T(8,128)} fusion(bf16[2,64,1,256]{3,1,2,0:T(8,128)(2,1)S(1)} %collective-permute-done.3, bf16[2,64,24,256]{3,1,2,0:T(8,128)(2,1)S(1)} %fusion.15, bf16[3,3,64,64]{3,2,1,0:T(8,128)(2,1)S(1)} %copy-done.1), kind=kOutput, calls=%fused_computation.83 | convolution fusion | flops 103809024 | bytes 4800512 | tf_op jit(solution)/shard_map/oc,pcxy->poxy/dot_general | solution.py:29
  109.3 5.9 %fusion.16 = bf16[2,64,24,256]{3,1,2,0:T(8,128)(2,1)S(1)} fusion(f32[2,24,256,64]{2,3,1,0:T(8,128)} %fusion.73, f32[2,24,256,64]{2,3,1,0:T(8,128)S(1)} %fusion.75, f32[2,24,256,64]{2,3,1,0:T(8,128)S(1)} %fusion.77, f32[2,24,256,64]{2,3,1,0:T(8,128)S(1)} %fusion.101, f32[2,24,256,64]{2,3,1,0:T(8,128)S(1)} %fusion.79, f32[2,24,256,64]{2,3,1,0:T(8,128)} %fusion.81, ...), kind=kOutput, calls=%fused_computation.28 | convolution fusion | flops 110886912 | bytes 28327936 | tf_op jit(solution)/shard_map/oc,pcxy->poxy/dot_general | solution.py:29
  115.9 3.3 %collective-permute-start.5 = (bf16[2,64,1,256]{3,1,2,0:T(8,128)(2,1)S(1)}, bf16[2,64,1,256]{3,1,2,0:T(8,128)(2,1)S(1)}, u32[]{:S(2)}, u32[]{:S(2)}) collective-permute-start(bf16[2,64,1,256]{3,1,2,0:T(8,128)(2,1)S(1)} %get-tuple-element.17), channel_id=1, source_target_pairs={{4,0},{8,4},{12,8},{0,12},{5,1},{9,5},{13,9},{1,13},{6,2},{10,6},{... | collective-permute-start | bytes 196616 | tf_op jit(solution)/shard_map/ppermute | solution.py:16
  123.2 2.5 %fusion.59 = f32[2,24,256,69]{2,3,1,0:T(8,128)} fusion(bf16[2,64,26,258]{3,1,2,0:T(8,128)(2,1)S(1)} %select_maximum_fusion, bf16[3,3,69,64]{2,3,1,0:T(8,128)(2,1)S(1)} %copy-done.2), kind=kOutput, calls=%fused_computation.70 | convolution fusion | flops 108527616 | bytes 4980736 | tf_op jit(solution)/shard_map/oc,pcxy->poxy/dot_general | solution.py:29
  125.7 2.6 %fusion.61 = f32[2,24,256,69]{2,3,1,0:T(8,128)} fusion(bf16[2,64,26,258]{3,1,2,0:T(8,128)(2,1)S(1)} %select_maximum_fusion, bf16[3,3,69,64]{2,3,1,0:T(8,128)(2,1)S(1)} %copy-done.2), kind=kOutput, calls=%fused_computation.72 | convolution fusion | flops 108527616 | bytes 4980736 | tf_op jit(solution)/shard_map/oc,pcxy->poxy/dot_general | solution.py:29
  128.2 2.5 %fusion.63 = f32[2,24,256,69]{2,3,1,0:T(8,128)} fusion(bf16[2,64,26,258]{3,1,2,0:T(8,128)(2,1)S(1)} %select_maximum_fusion, bf16[3,3,69,64]{2,3,1,0:T(8,128)(2,1)S(1)} %copy-done.2), kind=kOutput, calls=%fused_computation.74 | convolution fusion | flops 108527616 | bytes 4980736 | tf_op jit(solution)/shard_map/oc,pcxy->poxy/dot_general | solution.py:29
  130.8 2.5 %fusion.65 = f32[2,24,256,69]{2,3,1,0:T(8,128)} fusion(bf16[2,64,26,258]{3,1,2,0:T(8,128)(2,1)S(1)} %select_maximum_fusion, bf16[3,3,69,64]{2,3,1,0:T(8,128)(2,1)S(1)} %copy-done.2), kind=kOutput, calls=%fused_computation.76 | convolution fusion | flops 108527616 | bytes 4980736 | tf_op jit(solution)/shard_map/oc,pcxy->poxy/dot_general | solution.py:29
  133.3 2.4 %fusion.67 = f32[2,24,256,69]{2,3,1,0:T(8,128)} fusion(bf16[2,64,26,258]{3,1,2,0:T(8,128)(2,1)S(1)} %select_maximum_fusion, bf16[3,3,69,64]{2,3,1,0:T(8,128)(2,1)S(1)} %copy-done.2), kind=kOutput, calls=%fused_computation.78 | convolution fusion | flops 108527616 | bytes 4980736 | tf_op jit(solution)/shard_map/oc,pcxy->poxy/dot_general | solution.py:29
  135.7 2.4 %fusion.47 = f32[2,24,256,69]{2,3,1,0:T(8,128)} fusion(bf16[2,64,24,256]{3,1,2,0:T(8,128)(2,1)S(1)} %fusion.16, bf16[2,64,1,256]{3,1,2,0:T(8,128)(2,1)S(1)} %collective-permute-done.4, bf16[3,3,69,64]{2,3,1,0:T(8,128)(2,1)S(1)} %copy-done.2), kind=kOutput, calls=%fused_computation.60 | convolution fusion | flops 111804416 | bytes 5046272 | tf_op jit(solution)/shard_map/oc,pcxy->poxy/dot_general | solution.py:29
  138.1 2.4 %fusion.51 = f32[2,24,256,69]{2,3,1,0:T(8,128)} fusion(bf16[2,64,1,256]{3,1,2,0:T(8,128)(2,1)S(1)} %collective-permute-done.5, bf16[2,64,24,256]{3,1,2,0:T(8,128)(2,1)S(1)} %fusion.16, bf16[3,3,69,64]{2,3,1,0:T(8,128)(2,1)S(1)} %copy-done.2), kind=kOutput, calls=%fused_computation.64 | convolution fusion | flops 111804416 | bytes 5046272 | tf_op jit(solution)/shard_map/oc,pcxy->poxy/dot_general | solution.py:29
  140.5 10.1 %fusion.3 = bf16[2,69,24,256]{3,1,2,0:T(8,128)(2,1)S(1)} fusion(f32[2,24,256,69]{2,3,1,0:T(8,128)} %fusion.51, f32[2,24,256,69]{2,3,1,0:T(8,128)} %fusion.59, f32[2,24,256,69]{2,3,1,0:T(8,128)} %fusion.61, f32[2,24,256,69]{2,3,1,0:T(8,128)S(1)} %fusion.91, f32[2,24,256,69]{2,3,1,0:T(8,128)} %fusion.63, f32[2,24,256,69]{2,3,1,0:T(8,128)} %fusion.65, ...), kind=kOutput, calls=%fused_computation.11 | convolution fusion | flops 122941440 | bytes 34055168 | tf_op jit(solution)/shard_map/oc,pcxy->poxy/dot_general | solution.py:29
  (58 shorter events, 30.0 us)
Async XLA Ops:
  7.2 2.2 %copy-start = (bf16[2,69,24,256]{3,2,1,0:T(8,128)(2,1)S(1)}, bf16[2,69,24,256]{3,2,1,0:T(8,128)(2,1)}, u32[]{:S(2)}) copy-start(bf16[2,69,24,256]{3,2,1,0:T(8,128)(2,1)} %param.9) | copy-start | bytes 5087236
  7.2 2.1 %copy-start.5 = (s32[24,256]{1,0:T(8,128)S(1)}, s32[24,256]{1,0:T(8,128)}, u32[]{:S(2)}) copy-start(s32[24,256]{1,0:T(8,128)} %param.12) | copy-start | bytes 73732
  7.2 2.1 %copy-start.4 = (f32[24,256]{1,0:T(8,128)S(1)}, f32[24,256]{1,0:T(8,128)}, u32[]{:S(2)}) copy-start(f32[24,256]{1,0:T(8,128)} %param.11) | copy-start | bytes 73732
  7.2 54.4 %all-gather.2.cloned.1.call-start = ((), (), s32[]{:S(2)}) async-start(), calls=%async_computation | async-start | bytes 8478720 | tf_op jit(solution)/shard_map/all_gather | solution.py:55
  7.9 15.7 %copy-start.7 = (u32[32]{0:T(128)S(1)}, u32[32]{0:T(128)}, u32[]{:S(2)}) copy-start(u32[32]{0:T(128)} %constant.60) | copy-start | bytes 388
  7.9 28.4 %copy-start.6 = (s32[2]{0:T(128)S(1)}, s32[2]{0:T(128)}, u32[]{:S(2)}) copy-start(s32[2]{0:T(128)} %param.13) | copy-start | bytes 28
  65.2 4.4 %copy-start.3 = (bf16[3,3,64,69]{3,2,1,0:T(8,128)(2,1)S(1)}, bf16[3,3,64,69]{3,2,1,0:T(8,128)(2,1)}, u32[]{:S(2)}) copy-start(bf16[3,3,64,69]{3,2,1,0:T(8,128)(2,1)} %param.15) | copy-start | bytes 238468
  65.7 6.7 %collective-permute-start = (bf16[2,69,1,256]{3,1,2,0:T(8,128)(2,1)S(1)}, bf16[2,69,1,256]{3,1,2,0:T(8,128)(2,1)S(1)}, u32[]{:S(2)}, u32[]{:S(2)}) collective-permute-start(bf16[2,69,1,256]{3,1,2,0:T(8,128)(2,1)S(1)} %get-tuple-element.14), channel_id=1, source_target_pairs={{0,4},{4,8},{8,12},{12,0},{1,5},{5,9},{9,13},{13,1},{2,6},{6,10},{... | collective-permute-start | bytes 211976 | tf_op jit(solution)/shard_map/ppermute | solution.py:13
  67.2 5.7 %collective-permute-start.1 = (bf16[2,69,1,256]{3,1,2,0:T(8,128)(2,1)S(1)}, bf16[2,69,1,256]{3,1,2,0:T(8,128)(2,1)S(1)}, u32[]{:S(2)}, u32[]{:S(2)}) collective-permute-start(bf16[2,69,1,256]{3,1,2,0:T(8,128)(2,1)S(1)} %get-tuple-element.15), channel_id=1, source_target_pairs={{4,0},{8,4},{12,8},{0,12},{5,1},{9,5},{13,9},{1,13},{6,2},{10,6},{... | collective-permute-start | bytes 211976 | tf_op jit(solution)/shard_map/ppermute | solution.py:16
  84.4 9.9 %copy-start.1 = (bf16[3,3,64,64]{3,2,1,0:T(8,128)(2,1)S(1)}, bf16[3,3,64,64]{3,2,1,0:T(8,128)(2,1)}, u32[]{:S(2)}) copy-start(bf16[3,3,64,64]{3,2,1,0:T(8,128)(2,1)} %param.16) | copy-start | bytes 221188
  90.4 6.3 %collective-permute-start.2 = (bf16[2,64,1,256]{3,1,2,0:T(8,128)(2,1)S(1)}, bf16[2,64,1,256]{3,1,2,0:T(8,128)(2,1)S(1)}, u32[]{:S(2)}, u32[]{:S(2)}) collective-permute-start(bf16[2,64,1,256]{3,1,2,0:T(8,128)(2,1)S(1)} %get-tuple-element.18), channel_id=1, source_target_pairs={{0,4},{4,8},{8,12},{12,0},{1,5},{5,9},{9,13},{13,1},{2,6},{6,10},{... | collective-permute-start | bytes 196616 | tf_op jit(solution)/shard_map/ppermute | solution.py:13
  91.6 5.2 %collective-permute-start.3 = (bf16[2,64,1,256]{3,1,2,0:T(8,128)(2,1)S(1)}, bf16[2,64,1,256]{3,1,2,0:T(8,128)(2,1)S(1)}, u32[]{:S(2)}, u32[]{:S(2)}) collective-permute-start(bf16[2,64,1,256]{3,1,2,0:T(8,128)(2,1)S(1)} %get-tuple-element.19), channel_id=1, source_target_pairs={{4,0},{8,4},{12,8},{0,12},{5,1},{9,5},{13,9},{1,13},{6,2},{10,6},{... | collective-permute-start | bytes 196616 | tf_op jit(solution)/shard_map/ppermute | solution.py:16
  109.3 9.9 %copy-start.2 = (bf16[3,3,69,64]{2,3,1,0:T(8,128)(2,1)S(1)}, bf16[3,3,69,64]{2,3,1,0:T(8,128)(2,1)}, u32[]{:S(2)}) copy-start(bf16[3,3,69,64]{2,3,1,0:T(8,128)(2,1)} %param.17) | copy-start | bytes 238468
  115.3 6.2 %collective-permute-start.4 = (bf16[2,64,1,256]{3,1,2,0:T(8,128)(2,1)S(1)}, bf16[2,64,1,256]{3,1,2,0:T(8,128)(2,1)S(1)}, u32[]{:S(2)}, u32[]{:S(2)}) collective-permute-start(bf16[2,64,1,256]{3,1,2,0:T(8,128)(2,1)S(1)} %get-tuple-element.16), channel_id=1, source_target_pairs={{0,4},{4,8},{8,12},{12,0},{1,5},{5,9},{9,13},{13,1},{2,6},{6,10},{... | collective-permute-start | bytes 196616 | tf_op jit(solution)/shard_map/ppermute | solution.py:13
  115.9 5.6 %collective-permute-start.5 = (bf16[2,64,1,256]{3,1,2,0:T(8,128)(2,1)S(1)}, bf16[2,64,1,256]{3,1,2,0:T(8,128)(2,1)S(1)}, u32[]{:S(2)}, u32[]{:S(2)}) collective-permute-start(bf16[2,64,1,256]{3,1,2,0:T(8,128)(2,1)S(1)} %get-tuple-element.17), channel_id=1, source_target_pairs={{4,0},{8,4},{12,8},{0,12},{5,1},{9,5},{13,9},{1,13},{6,2},{10,6},{... | collective-permute-start | bytes 196616 | tf_op jit(solution)/shard_map/ppermute | solution.py:16
Sparse Core Ops, SparseCore 0:
  9.6 51.9 all-gather.1
where the time goes:
time: 159 us
  matrix products  63.2 us (40%)
  waiting for transfers between devices  30.2 us (19%)
  blocking collectives  19.6 us (12%)
  between operations  16.9 us (11%)
  starting transfers between devices  11.7 us (7%)
  other arithmetic  9.41 us (6%)
  local copies, waits for them, and re-layouts  7.92 us (5%)
    dot_general x27, matrix products, conv_local(): jnp.einsum('oc,pcxy->poxy', weight[row_tap, col_tap], window, preferred_e...  63.2 us
    all_gather x1, waiting for transfers between devices, continue_slots(): slab_piece = lax.all_gather(slabs, 'dom', axis=0, tiled=True)  25.2 us
    psum x1, blocking collectives, on_device(): band_sums = lax.psum(local_sums, 'lon')  13.4 us
    ppermute x3, starting transfers between devices, extended_2(): lax.ppermute(lax.slice_in_dim(block, 0, width, axis=dim), axis, backward)  8.36 us
    unnamed x1, blocking collectives  6.14 us
    concatenate x3, other arithmetic, extended_2(): block = jnp.concatenate([low, block, high], axis=dim)  5.59 us
    ppermute x3, waiting for transfers between devices, extended_2(): lax.ppermute(lax.slice_in_dim(block, block.shape[dim] - width, None, axis...  3.61 us
    gather x1, local copies, waits for them, and re-layouts, continue_slots(): jnp.take(slab_piece, jnp.clip(slot_ancestors, 0, piece_rows - 1), axis=0)  3.58 us
  transfers between devices with their start and end apart: 7, of which 6 were waited for; matrix products, arithmetic and copies ran while one was open for 6% of the time, Pallas kernels for 0%

commit v1 on v0

v1 whole, which is shorter than its diff:
```python
import functools

import jax
import jax.numpy as jnp
from jax import lax
from jax.experimental import pallas as pl
from jax.experimental.pallas import tpu as pltpu
from jax.sharding import PartitionSpec as P

CHUNKS = 2
UNROLL = 2


def pad_to(count, step):
    return -(-count // step) * step


def stacked_taps(weight, out_rows, in_rows):
    _, _, outs, ins = weight.shape
    w = jnp.pad(weight, ((0, 0), (0, 0), (0, out_rows - outs), (0, in_rows - ins)))
    return w.transpose(1, 2, 0, 3).reshape(3 * out_rows, 3 * in_rows)


def conv_column(src_ref, w, x, in_rows, out_rows, first, last):
    window = src_ref[pl.ds(pl.multiple_of(x * in_rows, in_rows), 3 * in_rows), :]
    p = jnp.dot(w, window, preferred_element_type=jnp.float32)
    lat = p.shape[1]
    below = pltpu.roll(p[:out_rows], 1, 1)
    above = pltpu.roll(p[2 * out_rows :], lat - 1, 1)
    return (
        p[out_rows : 2 * out_rows]
        + jnp.where(first, 0.0, below)
        + jnp.where(last, 0.0, above)
    )


def silu(v):
    half = 0.5 * v
    return half + half * jnp.tanh(half)


def step_kernel(cols, cin, hid, nvars, ext_ref, obs_ref, ow_ref, w1_ref, w2_ref, w3_ref, out_ref, a1, a2):
    lat = out_ref.shape[-1]
    lane_h = lax.broadcasted_iota(jnp.int32, (hid, lat), 1)
    lane_o = lax.broadcasted_iota(jnp.int32, (cin, lat), 1)
    first_h, last_h = lane_h == 0, lane_h == lat - 1
    first_o, last_o = lane_o == 0, lane_o == lat - 1
    ext = ext_ref.at[0]

    def one(x, _):
        v = conv_column(ext, w1_ref[...], x, cin, hid, first_h, last_h)
        a1[pl.ds(pl.multiple_of(x * hid, hid), hid), :] = silu(v).astype(jnp.bfloat16)
        return 0

    def two(x, _):
        v = conv_column(a1, w2_ref[...], x, hid, hid, first_h, last_h)
        a2[pl.ds(pl.multiple_of(x * hid, hid), hid), :] = silu(v).astype(jnp.bfloat16)
        return 0

    def three(x, _):
        noise = conv_column(a2, w3_ref[...], x, hid, cin, first_o, last_o)
        current = ext[pl.ds(pl.multiple_of((x + 3) * cin, cin), cin), :].astype(jnp.float32)
        seen = obs_ref[x].astype(jnp.float32)
        gain = 0.25 * ow_ref[x]
        new = current - 0.5 * noise + gain * (seen - current)
        out_ref[0, x] = new[:nvars].astype(jnp.bfloat16)
        return 0

    lax.fori_loop(0, cols + 4, one, 0, unroll=UNROLL)
    lax.fori_loop(0, cols + 2, two, 0, unroll=UNROLL)
    lax.fori_loop(0, cols, three, 0, unroll=UNROLL)


def update_chunk(ext, observed, obs_weight, w1, w2, w3, nvars, hid):
    slots, wide, cin, lat = ext.shape
    cols = wide - 6
    ext = ext.reshape(slots, wide * cin, lat)
    whole = lambda a: pl.BlockSpec(a.shape, lambda p: (0,) * a.ndim)
    flops = 2 * slots * lat * ((cols + 4) * w1.size + (cols + 2) * w2.size + cols * w3.size)
    return pl.pallas_call(
        functools.partial(step_kernel, cols, cin, hid, nvars),
        out_shape=jax.ShapeDtypeStruct((slots, cols, nvars, lat), jnp.bfloat16),
        grid=(slots,),
        in_specs=[
            pl.BlockSpec((1, wide * cin, lat), lambda p: (p, 0, 0)),
            whole(observed),
            whole(obs_weight),
            whole(w1),
            whole(w2),
            whole(w3),
        ],
        out_specs=pl.BlockSpec((1, cols, nvars, lat), lambda p: (p, 0, 0, 0)),
        scratch_shapes=[
            pltpu.VMEM(((cols + 4) * hid, lat), jnp.bfloat16),
            pltpu.VMEM(((cols + 2) * hid, lat), jnp.bfloat16),
        ],
        compiler_params=pltpu.CompilerParams(vmem_limit_bytes=32 << 20),
        cost_estimate=pl.CostEstimate(
            flops=flops, bytes_accessed=2 * (ext.size + observed.size + slots * cols * nvars * lat), transcendentals=0
        ),
        name="update_chunk",
    )(ext, observed, obs_weight, w1, w2, w3)


def resample_chunk(u, own_anc, sibling_anc):
    n = lax.axis_size("dom")
    slots = u.shape[0]
    chips = n // 2
    me = lax.axis_index("dom")
    chip, core = me // 2, me % 2
    pieces = [u] + [
        lax.ppermute(u, "dom", [(d, (d + 2 * k) % n) for d in range(n)]) for k in range(1, chips)
    ]

    def pick(a):
        owner = a // slots
        value = u[0]
        for k, piece in enumerate(pieces):
            here = owner // 2 == (chip - k + chips) % chips
            for j in range(slots):
                if k or j:
                    value = jnp.where(here & (a % slots == j), piece[j], value)
        return value

    sent = jnp.stack([pick(sibling_anc[s]) for s in range(slots)])
    received = lax.ppermute(sent, "dom", [(d, d ^ 1) for d in range(n)])
    return jnp.stack(
        [
            jnp.where((own_anc[s] // slots) % 2 == core, pick(own_anc[s]), received[s])
            for s in range(slots)
        ]
    )


def on_device(particles, observed, precision, stations, ancestors, tempering, w_in, w_mid, w_out):
    slots, nvars, cols, lat = particles.shape
    hid = w_mid.shape[2]
    cin = pad_to(nvars, 16)
    n_dom, n_lon = lax.axis_size("dom"), lax.axis_size("lon")

    by_column = jnp.pad(particles.transpose(0, 2, 1, 3), ((0, 0), (0, 0), (0, cin - nvars), (0, 0)))
    ahead = [(i, (i + 1) % n_lon) for i in range(n_lon)]
    back = [(t, s) for s, t in ahead]
    low = lax.ppermute(by_column[:, cols - 3 :], "lon", ahead)
    high = lax.ppermute(by_column[:, :3], "lon", back)
    ext = jnp.concatenate([low, by_column, high], axis=1)
    sibling_anc = lax.ppermute(ancestors, "dom", [(d, d ^ 1) for d in range(n_dom)])

    obs_weight = stations.astype(jnp.float32) * precision
    misfit_cell = particles.astype(jnp.float32) - observed.astype(jnp.float32)[None]
    local_sums = jnp.sum(obs_weight[None, None] * misfit_cell * misfit_cell, axis=(1, 2, 3))
    all_sums = lax.all_gather(local_sums, ("lon", "dom"))
    every_sum = jnp.sum(all_sums.reshape(n_lon, n_dom * slots), axis=0)
    center = jnp.mean(every_sum)
    deviation = every_sum - center
    spread = jnp.sqrt(jnp.mean(deviation * deviation) + 1.0)
    log_weights = -0.5 * tempering[0] * deviation / spread
    expo = jnp.exp(log_weights)
    weights_all = expo / jnp.sum(expo)
    own_weights = lax.dynamic_slice_in_dim(weights_all, lax.axis_index("dom") * slots, slots)

    obs_columns = jnp.pad(observed.transpose(1, 0, 2), ((0, 0), (0, cin - nvars), (0, 0)))
    ow_columns = obs_weight[:, None, :]
    w1 = stacked_taps(w_in, hid, cin)
    w2 = stacked_taps(w_mid, hid, hid)
    w3 = stacked_taps(w_out, cin, hid)

    step = cols // CHUNKS
    done = []
    for c in range(CHUNKS):
        lo, hi = c * step, cols if c == CHUNKS - 1 else (c + 1) * step
        u = update_chunk(
            ext[:, lo : hi + 6], obs_columns[lo:hi], ow_columns[lo:hi], w1, w2, w3, nvars, hid
        )
        done.append(resample_chunk(u, ancestors, sibling_anc))
    new_particles = jnp.concatenate(done, axis=1).transpose(0, 2, 1, 3)
    return (new_particles, own_weights)


def solution(mesh):
    return jax.shard_map(
        on_device,
        mesh=mesh,
        in_specs=(
            P(("ens", "dom"), None, "lon", None),
            P("ens", "lon", None),
            P(("ens", "lon"), None),
            P(("ens", "lon"), None),
            P(("ens", "dom")),
            P("ens"),
            P(),
            P(),
            P(),
        ),
        out_specs=(P(("ens", "dom"), None, "lon", None), P(("ens", "dom"))),
        check_vma=False,
    )
```

time: 159 us -> 139 us (0.87)
  matrix products: 63.2 us -> 0 us
  Pallas kernels: 0 us -> 26.3 us
  blocking collectives: 19.6 us -> 40.2 us
  local copies, waits for them, and re-layouts: 7.92 us -> 23.6 us
  waiting for transfers between devices: 30.2 us -> 14.9 us
  starting transfers between devices: 11.7 us -> 6.85 us
  other arithmetic: 9.41 us -> 12.7 us
  between operations: 16.9 us -> 14.2 us
    dot_general x27 -> x0, matrix products: 63.2 us -> none  [conv_local(): jnp.einsum('oc,pcxy->poxy', weight[row_tap, col_tap], window, preferred_e...]
    unnamed x1, blocking collectives: 6.14 us -> 40.2 us
    pallas_call x0 -> x2, Pallas kernels: none -> 26.3 us  [update_chunk(): pl.pallas_call(functools.partial(step_kernel, cols, cin, hid, nvars), out...]
    all_gather x1 -> x0, waiting for transfers between devices: 25.2 us -> none  [continue_slots(): slab_piece = lax.all_gather(slabs, 'dom', axis=0, tiled=True)]
    psum x1 -> x0, blocking collectives: 13.4 us -> none  [on_device(): band_sums = lax.psum(local_sums, 'lon')]
    slice x3 -> x13, local copies, waits for them, and re-layouts: 0.03 us -> 12.2 us  [the longest x2 4.13 us: pick(): value = jnp.where(here & (a % slots == j), piece[j], value)]
    ppermute x6 -> x7, waiting for transfers between devices: 4.29 us -> 14.9 us  [the longest x2 13.6 us: resample_chunk(): lax.ppermute(u, 'dom', [(d, (d + 2 * k) % n) for d in range(n)])]
    ppermute x6 -> x7, starting transfers between devices: 11.7 us -> 6.85 us  [the longest x1 2.59 us: on_device(): low = lax.ppermute(by_column[:, cols - 3:], 'lon', ahead)]
  transfers between devices with their start and end apart: 7 -> 7, of which waited for: 6 -> 2; matrix products, arithmetic and copies ran while one was open for 6% -> 24% of each run, Pallas kernels for 0% -> 19%
where the time goes in v1:
time: 139 us
  blocking collectives  40.2 us (29%)
  Pallas kernels  26.3 us (19%)
  local copies, waits for them, and re-layouts  23.6 us (17%)
  waiting for transfers between devices  14.9 us (11%)
  between operations  14.2 us (10%)
  other arithmetic  12.7 us (9%)
  starting transfers between devices  6.85 us (5%)
    unnamed x1, blocking collectives  40.2 us
    pallas_call x2, Pallas kernels, update_chunk(): pl.pallas_call(functools.partial(step_kernel, cols, cin, hid, nvars), out...  26.3 us
    ppermute x2, waiting for transfers between devices, resample_chunk(): lax.ppermute(u, 'dom', [(d, (d + 2 * k) % n) for d in range(n)])  13.6 us
    concatenate x1, other arithmetic, on_device(): ext = jnp.concatenate([low, by_column, high], axis=1)  5.29 us
    slice x2, local copies, waits for them, and re-layouts, pick(): value = jnp.where(here & (a % slots == j), piece[j], value)  4.13 us
    unnamed x23, local copies, waits for them, and re-layouts  3.88 us
  transfers between devices with their start and end apart: 7, of which 2 were waited for; matrix products, arithmetic and copies ran while one was open for 24% of the time, Pallas kernels for 19%

profile of v1, /device:TPU:0, one launch (start us, length us, event | category | flops | bytes accessed | tf_op | source)
XLA Modules:
  0.0 138.6 jit_solution(6929790066875877218)
XLA Ops:
  1.2 2.3 %pad_slice_fusion.3 = (bf16[2,3,80,256]{3,1,2,0:T(4,128)(2,1)}, bf16[2,3,80,256]{3,1,2,0:T(4,128)(2,1)}) fusion(bf16[2,24,69,256]{3,1,2,0:T(8,128)(2,1)} %bitcast.23), kind=kLoop, calls=%fused_computation.26 | loop fusion | bytes 2187264 | tf_op jit(solution)/shard_map/slice | solution.py:144
  3.5 2.6 %collective-permute-start = (bf16[2,3,80,256]{3,1,2,0:T(4,128)(2,1)}, bf16[2,3,80,256]{3,1,2,0:T(4,128)(2,1)}, u32[]{:S(2)}, u32[]{:S(2)}) collective-permute-start(bf16[2,3,80,256]{3,1,2,0:T(4,128)(2,1)} %get-tuple-element.22), channel_id=1, source_target_pairs={{0,4},{4,8},{8,12},{12,0},{1,5},{5,9},{9,13},{13,1},{2,6},{6,10},{... | collective-permute-start | bytes 737288 | tf_op jit(solution)/shard_map/ppermute | solution.py:144
  6.1 2.0 %collective-permute-start.4 = (bf16[2,3,80,256]{3,1,2,0:T(4,128)(2,1)}, bf16[2,3,80,256]{3,1,2,0:T(4,128)(2,1)}, u32[]{:S(2)}, u32[]{:S(2)}) collective-permute-start(bf16[2,3,80,256]{3,1,2,0:T(4,128)(2,1)} %get-tuple-element.23), channel_id=1, source_target_pairs={{4,0},{8,4},{12,8},{0,12},{5,1},{9,5},{13,9},{1,13},{6,2},{10,6},{... | collective-permute-start | bytes 737288 | tf_op jit(solution)/shard_map/ppermute | solution.py:145
  14.0 1.5 %copy.70 = bf16[69,24,256]{2,0,1:T(8,128)(2,1)S(1)} copy(bf16[69,24,256]{2,1,0:T(8,128)(2,1)} %param.10) | data formatting | bytes 1695744 | tf_op args[1]
  15.5 2.5 %convert_element_type.19 = f32[69,24,256]{2,1,0:T(8,128)} convert(bf16[69,24,256]{2,1,0:T(8,128)(2,1)} %param.10) | non-fusion elementwise | flops 423936 | bytes 2543616 | tf_op jit(solution)/shard_map/convert_element_type | solution.py:150
  18.0 1.4 pad.16
  21.9 1.3 collective-permute-done.4
  23.2 5.3 %pad_maximum_fusion.1 = (bf16[2,18,80,256]{3,1,2,0:T(8,128)(2,1)S(1)}, bf16[2,18,80,256]{3,1,2,0:T(8,128)(2,1)}) fusion(bf16[2,24,80,256]{3,1,2,0:T(8,128)(2,1)} %pad.16, bf16[2,3,80,256]{3,1,2,0:T(4,128)(2,1)} %collective-permute-done, bf16[2,3,80,256]{3,1,2,0:T(4,128)(2,1)} %collective-permute-done.4), kind=kLoop, calls=%fused_computation.3 | loop fusion | flops 5898240 | bytes 5406720 | tf_op jit(solution)/shard_map/concatenate | solution.py:146
  28.8 13.1 %update_chunk.2 = bf16[2,12,69,256]{3,2,1,0:T(8,128)(2,1)S(1)} custom-call(bf16[2,1440,256]{2,1,0:T(8,128)(2,1)S(1)} %bitcast.22, bf16[12,80,256]{2,1,0:T(8,128)(2,1)S(1)} %get-tuple-element.24.obs_ref, f32[12,1,256]{2,1,0:T(1,128)S(1)} %copy.34.ow_ref, bf16[192,240]{1,0:T(8,128)(2,1)S(1)} %reshape.29.w1_ref, bf16[192,192]{1,0:T(8,128)(2,1)S(1)} %reshape.30.w2_ref, ...), custom_call_target="tpu_custom_call" | custom-call | flops 1849688064 | bytes 2813952 | tf_op jit(solution)/shard_map/update_chunk/pallas_call | solution.py:80
  42.0 1.8 %copy.36 = bf16[2,12,69,256]{3,0,2,1:T(2,128)(2,1)} copy(bf16[2,12,69,256]{3,2,1,0:T(8,128)(2,1)S(1)} %update_chunk.2) | data formatting | bytes 1695744 | tf_op jit(solution)/shard_map/update_chunk/pallas_call | solution.py:80
  43.8 1.5 %collective-permute-start.1 = (bf16[2,12,69,256]{3,0,2,1:T(2,128)(2,1)}, bf16[2,12,69,256]{3,0,2,1:T(2,128)(2,1)}, u32[]{:S(2)}, u32[]{:S(2)}) collective-permute-start(bf16[2,12,69,256]{3,0,2,1:T(2,128)(2,1)} %copy.36), channel_id=1, source_target_pairs={{0,2},{1,3},{2,0},{3,1},{4,6},{5,7},{6,4},{7,5},{8,10},{9,11},{10,... | collective-permute-start | bytes 2543624 | tf_op jit(solution)/shard_map/ppermute | solution.py:112
  45.3 0.7 fusion
  46.2 40.2 %all-reduce.4 = f32[32]{0:T(128)S(1)} all-reduce(f32[32]{0:T(128)S(1)} %dynamic-update-slice), channel_id=2, replica_groups=mesh['ens'=2,'lon'=4,'dom'=4] {'lon','dom'}, use_global_device_ids=true, to_apply=%add.4 | all-reduce | flops 32 | bytes 256
  96.2 1.8 %copy.42 = bf16[2,18,80,256]{3,2,1,0:T(8,128)(2,1)S(1)} copy(bf16[2,18,80,256]{3,1,2,0:T(8,128)(2,1)} %get-tuple-element.17) | data formatting | bytes 2949120 | tf_op jit(solution)/shard_map/slice | solution.py:173
  98.1 13.2 %update_chunk.3 = bf16[2,12,69,256]{3,2,1,0:T(8,128)(2,1)S(1)} custom-call(bf16[2,1440,256]{2,1,0:T(8,128)(2,1)S(1)} %bitcast.21, bf16[12,80,256]{2,1,0:T(8,128)(2,1)S(1)} %get-tuple-element.25.obs_ref, f32[12,1,256]{2,1,0:T(1,128)S(1)} %slice.131.ow_ref, bf16[192,240]{1,0:T(8,128)(2,1)S(1)} %reshape.29.w1_ref, bf16[192,192]{1,0:T(8,128)(2,1)S(1)} %reshape.30.w2_ref, ...), custom_call_target="tpu_custom_call" | custom-call | flops 1849688064 | bytes 2813952 | tf_op jit(solution)/shard_map/update_chunk/pallas_call | solution.py:80
  111.3 0.9 copy.44
  112.2 3.0 %fusion.3 = (bf16[1,12,69,256]{3,0,2,1:T(2,128)(2,1)S(1)}, bf16[1,12,69,256]{3,0,2,1:T(2,128)(2,1)S(1)}) fusion(bf16[2,12,69,256]{3,0,2,1:T(2,128)(2,1)} %collective-permute-done.1), kind=kLoop, calls=%fused_computation.29 | loop fusion | bytes 1695744 | tf_op jit(solution)/shard_map/slice | solution.py:122
  115.6 0.9 copy.39
  116.6 13.6 %collective-permute-done.5 = bf16[2,12,69,256]{3,0,2,1:T(2,128)(2,1)S(1)} collective-permute-done((bf16[2,12,69,256]{3,0,2,1:T(2,128)(2,1)S(1)}, bf16[2,12,69,256]{3,0,2,1:T(2,128)(2,1)S(1)}, u32[]{:S(2)}, u32[]{:S(2)}) %collective-permute-start.5) | collective-permute-done | bytes 847904 | tf_op jit(solution)/shard_map/ppermute | solution.py:112
  130.2 1.2 fusion.5
  131.8 0.9 copy.47
  134.0 1.2 fusion.2
  135.5 1.2 fusion.4
  137.1 1.5 %copy.50 = bf16[2,69,24,256]{3,2,1,0:T(8,128)(2,1)} copy(bf16[2,69,24,256]{3,1,2,0:T(8,128)(2,1)S(1)} %maximum_bitcast_fusion) | data formatting | bytes 3391488
  (62 shorter events, 9.0 us)
Async XLA Ops:
  0.6 7.5 %copy-start.7 = (s32[2]{0:T(128)S(1)}, s32[2]{0:T(128)}, u32[]{:S(2)}) copy-start(s32[2]{0:T(128)} %param.13) | copy-start | bytes 28
  0.6 89.7 %collective-permute-start.2 = (s32[2]{0:T(128)}, s32[2]{0:T(128)S(1)}, u32[]{:S(2)}, u32[]{:S(2)}) collective-permute-start(s32[2]{0:T(128)} %param.13), channel_id=1, source_target_pairs={{0,1},{1,0},{2,3},{3,2},{4,5},{5,4},{6,7},{7,6},{8,9},{9,8},{10,11... | collective-permute-start | bytes 32 | tf_op jit(solution)/shard_map/ppermute | solution.py:147
  3.5 18.4 %collective-permute-start = (bf16[2,3,80,256]{3,1,2,0:T(4,128)(2,1)}, bf16[2,3,80,256]{3,1,2,0:T(4,128)(2,1)}, u32[]{:S(2)}, u32[]{:S(2)}) collective-permute-start(bf16[2,3,80,256]{3,1,2,0:T(4,128)(2,1)} %get-tuple-element.22), channel_id=1, source_target_pairs={{0,4},{4,8},{8,12},{12,0},{1,5},{5,9},{9,13},{13,1},{2,6},{6,10},{... | collective-permute-start | bytes 737288 | tf_op jit(solution)/shard_map/ppermute | solution.py:144
  6.1 17.2 %collective-permute-start.4 = (bf16[2,3,80,256]{3,1,2,0:T(4,128)(2,1)}, bf16[2,3,80,256]{3,1,2,0:T(4,128)(2,1)}, u32[]{:S(2)}, u32[]{:S(2)}) collective-permute-start(bf16[2,3,80,256]{3,1,2,0:T(4,128)(2,1)} %get-tuple-element.23), channel_id=1, source_target_pairs={{4,0},{8,4},{12,8},{0,12},{5,1},{9,5},{13,9},{1,13},{6,2},{10,6},{... | collective-permute-start | bytes 737288 | tf_op jit(solution)/shard_map/ppermute | solution.py:145
  14.0 3.9 %copy-start = (bf16[2,69,24,256]{3,2,1,0:T(8,128)(2,1)S(1)}, bf16[2,69,24,256]{3,2,1,0:T(8,128)(2,1)}, u32[]{:S(2)}) copy-start(bf16[2,69,24,256]{3,2,1,0:T(8,128)(2,1)} %param.9) | copy-start | bytes 5087236
  17.9 1.4 %copy-start.5 = (f32[24,256]{1,0:T(8,128)S(1)}, f32[24,256]{1,0:T(8,128)}, u32[]{:S(2)}) copy-start(f32[24,256]{1,0:T(8,128)} %param.11) | copy-start | bytes 73732
  17.9 1.4 %copy-start.6 = (s32[24,256]{1,0:T(8,128)S(1)}, s32[24,256]{1,0:T(8,128)}, u32[]{:S(2)}) copy-start(s32[24,256]{1,0:T(8,128)} %param.12) | copy-start | bytes 73732
  17.9 1.5 %copy-start.2 = (bf16[3,3,69,64]{2,3,1,0:T(8,128)(2,1)S(1)}, bf16[3,3,69,64]{2,3,1,0:T(8,128)(2,1)}, u32[]{:S(2)}) copy-start(bf16[3,3,69,64]{2,3,1,0:T(8,128)(2,1)} %param.17) | copy-start | bytes 238468
  18.0 1.9 %copy-start.3 = (bf16[3,3,64,69]{3,2,1,0:T(8,128)(2,1)S(1)}, bf16[3,3,64,69]{3,2,1,0:T(8,128)(2,1)}, u32[]{:S(2)}) copy-start(bf16[3,3,64,69]{3,2,1,0:T(8,128)(2,1)} %param.15) | copy-start | bytes 238468
  19.4 0.9 copy-start.4
  19.4 1.2 copy-start.8
  42.0 3.3 %copy-start.1 = (f32[69,24,256]{2,1,0:T(8,128)S(1)}, f32[69,24,256]{2,1,0:T(8,128)}, u32[]{:S(2)}) copy-start(f32[69,24,256]{2,1,0:T(8,128)} %convert_element_type.19) | copy-start | bytes 5087236
  43.8 68.5 %collective-permute-start.1 = (bf16[2,12,69,256]{3,0,2,1:T(2,128)(2,1)}, bf16[2,12,69,256]{3,0,2,1:T(2,128)(2,1)}, u32[]{:S(2)}, u32[]{:S(2)}) collective-permute-start(bf16[2,12,69,256]{3,0,2,1:T(2,128)(2,1)} %copy.36), channel_id=1, source_target_pairs={{0,2},{1,3},{2,0},{3,1},{4,6},{5,7},{6,4},{7,5},{8,10},{9,11},{10,... | collective-permute-start | bytes 2543624 | tf_op jit(solution)/shard_map/ppermute | solution.py:112
  112.2 18.0 %collective-permute-start.5 = (bf16[2,12,69,256]{3,0,2,1:T(2,128)(2,1)S(1)}, bf16[2,12,69,256]{3,0,2,1:T(2,128)(2,1)S(1)}, u32[]{:S(2)}, u32[]{:S(2)}) collective-permute-start(bf16[2,12,69,256]{3,0,2,1:T(2,128)(2,1)S(1)} %copy.44), channel_id=1, source_target_pairs={{0,2},{1,3},{2,0},{3,1},{4,6},{5,7},{6,4},{7,5},{8,10},{9,11},{10,... | collective-permute-start | bytes 2543624 | tf_op jit(solution)/shard_map/ppermute | solution.py:112
  116.5 17.5 %collective-permute-start.3 = (bf16[2,12,69,256]{3,0,2,1:T(2,128)(2,1)S(1)}, bf16[2,12,69,256]{3,0,2,1:T(2,128)(2,1)S(1)}, u32[]{:S(2)}, u32[]{:S(2)}) collective-permute-start(bf16[2,12,69,256]{3,0,2,1:T(2,128)(2,1)S(1)} %copy.39), channel_id=1, source_target_pairs={{0,1},{1,0},{2,3},{3,2},{4,5},{5,4},{6,7},{7,6},{8,9},{9,8},{10,11... | collective-permute-start | bytes 2543624 | tf_op jit(solution)/shard_map/ppermute | solution.py:126
  132.7 2.8 %collective-permute-start.6 = (bf16[2,12,69,256]{3,0,2,1:T(2,128)(2,1)S(1)}, bf16[2,12,69,256]{3,0,2,1:T(2,128)(2,1)S(1)}, u32[]{:S(2)}, u32[]{:S(2)}) collective-permute-start(bf16[2,12,69,256]{3,0,2,1:T(2,128)(2,1)S(1)} %copy.47), channel_id=1, source_target_pairs={{0,1},{1,0},{2,3},{3,2},{4,5},{5,4},{6,7},{7,6},{8,9},{9,8},{10,11... | collective-permute-start | bytes 2543624 | tf_op jit(solution)/shard_map/ppermute | solution.py:126

commit v2 on v1

v2 whole, which is shorter than its diff:
```python
import functools

import jax
import jax.numpy as jnp
from jax import lax
from jax.experimental import pallas as pl
from jax.experimental.pallas import tpu as pltpu
from jax.sharding import PartitionSpec as P

CHUNKS = 3
UNROLL = True


def pad_to(count, step):
    return -(-count // step) * step


def stacked_taps(weight, out_rows, in_rows):
    _, _, outs, ins = weight.shape
    w = jnp.pad(weight, ((0, 0), (0, 0), (0, out_rows - outs), (0, in_rows - ins)))
    return w.transpose(1, 2, 0, 3).reshape(3 * out_rows, 3 * in_rows)


def conv_column(src_ref, w, x, in_rows, out_rows, first, last):
    window = src_ref[pl.ds(pl.multiple_of(x * in_rows, in_rows), 3 * in_rows), :]
    p = jnp.dot(w, window, preferred_element_type=jnp.float32)
    lat = p.shape[1]
    below = pltpu.roll(p[:out_rows], 1, 1)
    above = pltpu.roll(p[2 * out_rows :], lat - 1, 1)
    return (
        p[out_rows : 2 * out_rows]
        + jnp.where(first, 0.0, below)
        + jnp.where(last, 0.0, above)
    )


def silu(v):
    half = 0.5 * v
    return half + half * jnp.tanh(half)


def step_kernel(lo, hi, cin, hid, low_ref, mid_ref, high_ref, obs_ref, ow_ref, w1_ref, w2_ref, w3_ref, out_ref, ext, a1, a2):
    cols, nvars, lat = mid_ref.shape[1:]
    lane_h = lax.broadcasted_iota(jnp.int32, (hid, lat), 1)
    lane_o = lax.broadcasted_iota(jnp.int32, (cin, lat), 1)
    first_h, last_h = lane_h == 0, lane_h == lat - 1
    first_o, last_o = lane_o == 0, lane_o == lat - 1

    @pl.when(pl.program_id(0) == 0)
    def _():
        ext[...] = jnp.zeros_like(ext)

    for k, x in enumerate(range(lo - 3, hi + 3)):
        if x < 0:
            column = low_ref[0, x + 3]
        elif x >= cols:
            column = high_ref[0, x - cols]
        else:
            column = mid_ref[0, x]
        ext[k * cin : k * cin + nvars, :] = column

    def one(x, _):
        v = conv_column(ext, w1_ref[...], x, cin, hid, first_h, last_h)
        a1[pl.ds(pl.multiple_of(x * hid, hid), hid), :] = silu(v).astype(jnp.bfloat16)
        return 0

    def two(x, _):
        v = conv_column(a1, w2_ref[...], x, hid, hid, first_h, last_h)
        a2[pl.ds(pl.multiple_of(x * hid, hid), hid), :] = silu(v).astype(jnp.bfloat16)
        return 0

    def three(x, _):
        noise = conv_column(a2, w3_ref[...], x, hid, cin, first_o, last_o)[:nvars]
        current = ext[pl.ds(pl.multiple_of((x + 3) * cin, cin), cin), :].astype(jnp.float32)[:nvars]
        seen = obs_ref[lo + x].astype(jnp.float32)
        gain = 0.25 * ow_ref[lo + x]
        new = current - 0.5 * noise + gain * (seen - current)
        out_ref[0, x] = new.astype(jnp.bfloat16)
        return 0

    step = hi - lo
    lax.fori_loop(0, step + 4, one, 0, unroll=UNROLL)
    lax.fori_loop(0, step + 2, two, 0, unroll=UNROLL)
    lax.fori_loop(0, step, three, 0, unroll=UNROLL)


def update_chunk(lo, hi, low, mid, high, observed, obs_weight, w1, w2, w3, cin, hid):
    slots, _, nvars, lat = mid.shape
    step = hi - lo
    whole = lambda a: pl.BlockSpec(a.shape, lambda p: (0,) * a.ndim)
    own = lambda a: pl.BlockSpec((1,) + a.shape[1:], lambda p: (p, 0, 0, 0))
    flops = 2 * slots * lat * ((step + 4) * w1.size + (step + 2) * w2.size + step * w3.size)
    return pl.pallas_call(
        functools.partial(step_kernel, lo, hi, cin, hid),
        out_shape=jax.ShapeDtypeStruct((slots, step, nvars, lat), jnp.bfloat16),
        grid=(slots,),
        in_specs=[own(low), own(mid), own(high)]
        + [whole(a) for a in (observed, obs_weight, w1, w2, w3)],
        out_specs=pl.BlockSpec((1, step, nvars, lat), lambda p: (p, 0, 0, 0)),
        scratch_shapes=[
            pltpu.VMEM(((step + 6) * cin, lat), jnp.bfloat16),
            pltpu.VMEM(((step + 4) * hid, lat), jnp.bfloat16),
            pltpu.VMEM(((step + 2) * hid, lat), jnp.bfloat16),
        ],
        compiler_params=pltpu.CompilerParams(vmem_limit_bytes=24 << 20),
        cost_estimate=pl.CostEstimate(
            flops=flops * 8, bytes_accessed=2 * (mid.size + observed.size + slots * step * nvars * lat), transcendentals=0
        ),
        name="update_chunk",
    )(low, mid, high, observed, obs_weight, w1, w2, w3)


def exchange_kernel(n_lon, n_dom, mid_ref, sums_ref, low_ref, high_ref, all_ref, parts, total, edge_send, edge_recv, lon_send, lon_recv, dom_send, dom_recv):
    lon, dom = lax.axis_index("lon"), lax.axis_index("dom")
    cols = mid_ref.shape[1]

    def lon_at(k):
        return {"lon": lax.rem(lon + k, n_lon)}

    def dom_at(k):
        return {"dom": lax.rem(dom + k, n_dom)}

    barrier = pltpu.get_barrier_semaphore()
    for k in range(1, n_lon):
        pl.semaphore_signal(barrier, inc=1, device_id=lon_at(k), device_id_type=pl.DeviceIdType.MESH)
    for k in range(1, n_dom):
        pl.semaphore_signal(barrier, inc=1, device_id=dom_at(k), device_id_type=pl.DeviceIdType.MESH)
    pl.semaphore_wait(barrier, n_lon + n_dom - 2)

    def send(src, dst, s, r, target):
        copy = pltpu.make_async_remote_copy(
            src_ref=src, dst_ref=dst, send_sem=s, recv_sem=r,
            device_id=target, device_id_type=pl.DeviceIdType.MESH,
        )
        copy.start()
        return copy

    edges = [
        send(mid_ref.at[:, cols - 3 : cols], low_ref, edge_send.at[0], edge_recv.at[0], lon_at(1)),
        send(mid_ref.at[:, 0:3], high_ref, edge_send.at[1], edge_recv.at[1], lon_at(n_lon - 1)),
    ]
    parts[lon] = sums_ref[...]
    over_lon = [
        send(sums_ref, parts.at[lon], lon_send.at[k - 1], lon_recv.at[k - 1], lon_at(k))
        for k in range(1, n_lon)
    ]
    for copy in over_lon:
        copy.wait()
    band_sum = parts[0]
    for k in range(1, n_lon):
        band_sum = band_sum + parts[k]
    total[...] = band_sum
    all_ref[dom] = band_sum
    over_dom = [
        send(total, all_ref.at[dom], dom_send.at[k - 1], dom_recv.at[k - 1], dom_at(k))
        for k in range(1, n_dom)
    ]
    for copy in over_dom + edges:
        copy.wait()


def exchange(mid, sums, n_lon, n_dom):
    slots, _, nvars, lat = mid.shape
    edge = jax.ShapeDtypeStruct((slots, 3, nvars, lat), mid.dtype)
    vmem = pl.BlockSpec(memory_space=pltpu.VMEM)
    return pl.pallas_call(
        functools.partial(exchange_kernel, n_lon, n_dom),
        out_shape=(edge, edge, jax.ShapeDtypeStruct((n_dom,) + sums.shape, jnp.float32)),
        in_specs=[pl.BlockSpec(memory_space=pl.ANY), vmem],
        out_specs=(vmem, vmem, vmem),
        scratch_shapes=[
            pltpu.VMEM((n_lon,) + sums.shape, jnp.float32),
            pltpu.VMEM(sums.shape, jnp.float32),
            pltpu.SemaphoreType.DMA((2,)),
            pltpu.SemaphoreType.DMA((2,)),
            pltpu.SemaphoreType.DMA((n_lon - 1,)),
            pltpu.SemaphoreType.DMA((n_lon - 1,)),
            pltpu.SemaphoreType.DMA((n_dom - 1,)),
            pltpu.SemaphoreType.DMA((n_dom - 1,)),
        ],
        compiler_params=pltpu.CompilerParams(collective_id=0, has_side_effects=True),
        name="exchange",
    )(mid, sums)


def resample_chunk(u, candidate, here):
    n = lax.axis_size("dom")
    slots = u.shape[0]
    pieces = [u] + [
        lax.ppermute(u, "dom", [(d, (d + 2 * k) % n) for d in range(n)]) for k in range(1, n // 2)
    ]

    def pick(c):
        value = u[0]
        for m in range(1, len(pieces) * slots):
            value = jnp.where(c == m, pieces[m // slots][m % slots], value)
        return value

    sent = jnp.stack([pick(candidate[slots + s]) for s in range(slots)])
    received = lax.ppermute(sent, "dom", [(d, d ^ 1) for d in range(n)])
    return jnp.stack([jnp.where(here[s], pick(candidate[s]), received[s]) for s in range(slots)])


def on_device(particles, observed, precision, stations, ancestors, tempering, w_in, w_mid, w_out):
    slots, nvars, cols, lat = particles.shape
    hid = w_mid.shape[2]
    cin = pad_to(nvars, 16)
    n_dom, n_lon = lax.axis_size("dom"), lax.axis_size("lon")
    me = lax.axis_index("dom")
    mid = particles.transpose(0, 2, 1, 3)
    sibling_anc = lax.ppermute(ancestors, "dom", [(d, d ^ 1) for d in range(n_dom)])

    obs_weight = stations.astype(jnp.float32) * precision
    misfit_cell = particles.astype(jnp.float32) - observed.astype(jnp.float32)[None]
    local_sums = jnp.sum(obs_weight[None, None] * misfit_cell * misfit_cell, axis=(1, 2))
    sums = jnp.sum(local_sums.reshape(slots, lat // 128, 128), axis=1)
    sums = jnp.pad(sums, ((0, pad_to(slots, 8) - slots), (0, 0)))
    low, high, all_sums = exchange(mid, sums, n_lon, n_dom)
    every_sum = jnp.sum(all_sums[:, :slots], axis=2).reshape(n_dom * slots)
    center = jnp.mean(every_sum)
    deviation = every_sum - center
    spread = jnp.sqrt(jnp.mean(deviation * deviation) + 1.0)
    log_weights = -0.5 * tempering[0] * deviation / spread
    expo = jnp.exp(log_weights)
    weights_all = expo / jnp.sum(expo)
    own_weights = lax.dynamic_slice_in_dim(weights_all, me * slots, slots)

    wanted = jnp.concatenate([ancestors, sibling_anc])
    owner = lax.div(wanted, slots)
    chips = n_dom // 2
    steps = lax.rem(lax.shift_right_logical(me, 1) - lax.div(owner, 2) + chips, chips)
    candidate = steps * slots + lax.rem(wanted, slots)
    here = lax.rem(owner, 2) == (me & 1)

    obs_columns = observed.transpose(1, 0, 2)
    ow_columns = obs_weight[:, None, :]
    w1 = stacked_taps(w_in, hid, cin)
    w2 = stacked_taps(w_mid, hid, hid)
    w3 = stacked_taps(w_out, cin, hid)

    bounds = [cols * c // CHUNKS for c in range(CHUNKS + 1)]
    done = []
    for lo, hi in zip(bounds, bounds[1:]):
        u = update_chunk(lo, hi, low, mid, high, obs_columns, ow_columns, w1, w2, w3, cin, hid)
        done.append(resample_chunk(u, candidate, here))
    new_particles = jnp.concatenate(done, axis=1).transpose(0, 2, 1, 3)
    return (new_particles, own_weights)


def solution(mesh):
    return jax.shard_map(
        on_device,
        mesh=mesh,
        in_specs=(
            P(("ens", "dom"), None, "lon", None),
            P("ens", "lon", None),
            P(("ens", "lon"), None),
            P(("ens", "lon"), None),
            P(("ens", "dom")),
            P("ens"),
            P(),
            P(),
            P(),
        ),
        out_specs=(P(("ens", "dom"), None, "lon", None), P(("ens", "dom"))),
        check_vma=False,
    )
```

time: 139 us -> 88.4 us (0.64)
  blocking collectives: 40.2 us -> 0 us
  waiting for transfers between devices: 14.9 us -> 10.1 us
  between operations: 14.2 us -> 10.3 us
  Pallas kernels: 26.3 us -> 30.1 us
  starting transfers between devices: 6.85 us -> 4.73 us
  other arithmetic: 12.7 us -> 10.7 us
  local copies, waits for them, and re-layouts: 23.6 us -> 21.8 us
    unnamed x1 -> x0, blocking collectives: 40.2 us -> none
    unnamed x23 -> x47, local copies, waits for them, and re-layouts: 3.88 us -> 11.9 us
    slice x11 -> x5, local copies, waits for them, and re-layouts: 9.85 us -> 3.53 us  [the longest x3 2.2 us: pick(): value = jnp.where(c == m, pieces[m // slots][m % slots], value)]
    concatenate x1 -> x0, other arithmetic: 5.29 us -> none  [on_device(): ext = jnp.concatenate([low, by_column, high], axis=1)]
    ppermute x2 -> x0, starting transfers between devices: 4.62 us -> none  [the longest x1 2.59 us: on_device(): low = lax.ppermute(by_column[:, cols - 3:], 'lon', ahead)]
    pallas_call x2 -> x4, Pallas kernels: 26.3 us -> 30.1 us  [the longest x1 21 us: exchange(): pl.pallas_call(functools.partial(exchange_kernel, n_lon, n_dom), out_shap...]
    select_n x6, other arithmetic: 1.28 us -> 4.89 us  [the longest x3 4.46 us: resample_chunk(): jnp.where(here[s], pick(candidate[s]), received[s])]
    ppermute x2 -> x3, waiting for transfers between devices: 13.6 us -> 10.1 us  [resample_chunk(): lax.ppermute(u, 'dom', [(d, (d + 2 * k) % n) for d in range(n)])]
  transfers between devices with their start and end apart: 7 -> 7, of which waited for: 2 -> 1; matrix products, arithmetic and copies ran while one was open for 24% -> 25% of each run, Pallas kernels for 19% -> 34%
where the time goes in v2:
time: 88.4 us; the launch traced here: 87.7 us
  Pallas kernels  30.1 us (34%)
  local copies, waits for them, and re-layouts  21.8 us (25%)
  other arithmetic  10.7 us (12%)
  between operations  10.3 us (12%)
  waiting for transfers between devices  10.1 us (11%)
  starting transfers between devices  4.73 us (5%)
    pallas_call x1, Pallas kernels, exchange(): pl.pallas_call(functools.partial(exchange_kernel, n_lon, n_dom), out_shap...  21 us
    unnamed x47, local copies, waits for them, and re-layouts  11.9 us
    ppermute x3, waiting for transfers between devices, resample_chunk(): lax.ppermute(u, 'dom', [(d, (d + 2 * k) % n) for d in range(n)])  10.1 us
    pallas_call x3, Pallas kernels, update_chunk(): pl.pallas_call(functools.partial(step_kernel, lo, hi, cin, hid), out_shap...  9.11 us
    select_n x3, other arithmetic, resample_chunk(): jnp.where(here[s], pick(candidate[s]), received[s])  4.46 us
    ppermute x3, starting transfers between devices, resample_chunk(): lax.ppermute(u, 'dom', [(d, (d + 2 * k) % n) for d in range(n)])  3.5 us
    slice x3, local copies, waits for them, and re-layouts, pick(): value = jnp.where(c == m, pieces[m // slots][m % slots], value)  2.2 us
    pallas_call x3, local copies, waits for them, and re-layouts, update_chunk(): pl.pallas_call(functools.partial(step_kernel, lo, hi, cin, hid), out_shap...  1.95 us
  transfers between devices with their start and end apart: 7, of which 1 were waited for; matrix products, arithmetic and copies ran while one was open for 25% of the time, Pallas kernels for 34%

profile of v2, /device:TPU:0, one launch (start us, length us, event | category | flops | bytes accessed | tf_op | source)
XLA Modules:
  0.0 87.7 jit_solution(8592336837241237665)
XLA Ops:
  1.2 1.3 %copy.127 = bf16[69,24,256]{2,0,1:T(8,128)(2,1)S(1)} copy(bf16[69,24,256]{2,1,0:T(8,128)(2,1)} %param.10) | data formatting | bytes 1695744 | tf_op args[1]
  2.6 1.3 %convert_element_type.17 = f32[69,24,256]{2,1,0:T(8,128)} convert(bf16[69,24,256]{2,1,0:T(8,128)(2,1)S(1)} %copy-done.16) | non-fusion elementwise | flops 423936 | bytes 2543616 | tf_op jit(solution)/shard_map/convert_element_type | solution.py:214
  4.7 1.1 %copy.56 = bf16[3,64,3,64]{3,2,1,0:T(4,128)(2,1)S(1)} copy(bf16[3,64,3,64]{3,1,0,2:T(8,128)(2,1)} %bitcast.35) | data formatting | bytes 147456 | tf_op jit(solution)/shard_map/transpose | solution.py:21
  6.6 1.6 %copy.126 = bf16[2,69,24,256]{3,1,2,0:T(8,128)(2,1)} copy(bf16[2,69,24,256]{3,2,1,0:T(8,128)(2,1)S(1)} %copy-done.14) | data formatting | bytes 3391488 | tf_op args[0]
  10.4 21.0 %exchange.1 = (bf16[2,3,69,256]{3,2,1,0:T(8,128)(2,1)}, bf16[2,3,69,256]{3,2,1,0:T(8,128)(2,1)}, f32[4,8,128]{2,1,0:T(8,128)}) custom-call(bf16[2,24,69,256]{3,2,1,0:T(8,128)(2,1)} %bitcast.28, f32[8,128]{1,0:T(8,128)} %pad.12.sums_ref), custom_call_target="tpu_custom_call" | custom-call | tf_op jit(solution)/shard_map/exchange/pallas_call | solution.py:166
  32.3 0.9 %copy-done.11 = bf16[2,3,69,256]{3,2,1,0:T(8,128)(2,1)S(1)} copy-done((bf16[2,3,69,256]{3,2,1,0:T(8,128)(2,1)S(1)}, bf16[2,3,69,256]{3,2,1,0:T(8,128)(2,1)}, u32[]{:S(2)}) %copy-start.11) | copy-done | bytes 211992
  33.2 0.9 %copy-done.12 = bf16[2,3,69,256]{3,2,1,0:T(8,128)(2,1)S(1)} copy-done((bf16[2,3,69,256]{3,2,1,0:T(8,128)(2,1)S(1)}, bf16[2,3,69,256]{3,2,1,0:T(8,128)(2,1)}, u32[]{:S(2)}) %copy-start.12) | copy-done | bytes 211992
  34.2 3.0 %update_chunk.5 = bf16[2,8,69,256]{3,2,1,0:T(8,128)(2,1)S(1)} custom-call(bf16[2,3,69,256]{3,2,1,0:T(8,128)(2,1)S(1)} %copy-done.11, bf16[2,24,69,256]{3,2,1,0:T(8,128)(2,1)S(1)} %bitcast.29, bf16[2,3,69,256]{3,2,1,0:T(8,128)(2,1)S(1)} %copy-done.12, bf16[24,69,256]{2,1,0:T(8,128)(2,1)S(1)} %bitcast.32, f32[24,1,256]{2,1,0:T(1,128)S(1)} %broadcast_in_dim.2.ow_ref, ...), custom_call_target="tpu_custom_call" | custom-call | flops 10569646080 | bytes 3108864 | tf_op jit(solution)/shard_map/update_chunk/pallas_call | solution.py:93
  37.2 0.9 %copy.73 = bf16[2,8,69,256]{3,1,2,0:T(8,128)(2,1)} copy(bf16[2,8,69,256]{3,2,1,0:T(8,128)(2,1)S(1)} %update_chunk.5) | data formatting | bytes 1130496 | tf_op jit(solution)/shard_map/update_chunk/pallas_call | solution.py:93
  38.1 1.4 %collective-permute-start.5 = (bf16[2,8,69,256]{3,1,2,0:T(8,128)(2,1)}, bf16[2,8,69,256]{3,1,2,0:T(8,128)(2,1)}, u32[]{:S(2)}, u32[]{:S(2)}) collective-permute-start(bf16[2,8,69,256]{3,1,2,0:T(8,128)(2,1)} %copy.73), channel_id=1, source_target_pairs={{0,2},{1,3},{2,0},{3,1},{4,6},{5,7},{6,4},{7,5},{8,10},{9,11},{10,... | collective-permute-start | bytes 1695752 | tf_op jit(solution)/shard_map/ppermute | solution.py:190
  39.6 1.2 %copy-done.2 = bf16[69,24,256]{2,0,1:T(8,128)(2,1)S(1)} copy-done((bf16[69,24,256]{2,0,1:T(8,128)(2,1)S(1)}, bf16[69,24,256]{2,0,1:T(8,128)(2,1)}, u32[]{:S(2)}) %copy-start.2) | copy-done | bytes 847896
  40.7 3.0 %update_chunk.4 = bf16[2,8,69,256]{3,2,1,0:T(8,128)(2,1)S(1)} custom-call(bf16[2,3,69,256]{3,2,1,0:T(8,128)(2,1)S(1)} %copy-done.11, bf16[2,24,69,256]{3,2,1,0:T(8,128)(2,1)S(1)} %bitcast.30, bf16[2,3,69,256]{3,2,1,0:T(8,128)(2,1)S(1)} %copy-done.12, bf16[24,69,256]{2,1,0:T(8,128)(2,1)S(1)} %bitcast.33, f32[24,1,256]{2,1,0:T(1,128)S(1)} %broadcast_in_dim.2.ow_ref, ...), custom_call_target="tpu_custom_call" | custom-call | flops 10569646080 | bytes 3108864 | tf_op jit(solution)/shard_map/update_chunk/pallas_call | solution.py:93
  43.8 0.9 %copy.66 = bf16[2,8,69,256]{3,1,2,0:T(8,128)(2,1)} copy(bf16[2,8,69,256]{3,2,1,0:T(8,128)(2,1)S(1)} %update_chunk.4) | data formatting | bytes 1130496 | tf_op jit(solution)/shard_map/update_chunk/pallas_call | solution.py:93
  45.3 0.9 %copy-done.4 = bf16[240,192]{1,0:T(8,128)(2,1)S(1)} copy-done((bf16[240,192]{1,0:T(8,128)(2,1)S(1)}, bf16[240,192]{1,0:T(8,128)(2,1)}, u32[]{:S(2)}) %copy-start.4) | copy-done | bytes 92184
  47.9 3.0 %update_chunk.3 = bf16[2,8,69,256]{3,2,1,0:T(8,128)(2,1)S(1)} custom-call(bf16[2,3,69,256]{3,2,1,0:T(8,128)(2,1)S(1)} %copy-done.11, bf16[2,24,69,256]{3,2,1,0:T(8,128)(2,1)S(1)} %bitcast.31, bf16[2,3,69,256]{3,2,1,0:T(8,128)(2,1)S(1)} %copy-done.12, bf16[24,69,256]{2,1,0:T(8,128)(2,1)S(1)} %bitcast.34, f32[24,1,256]{2,1,0:T(1,128)S(1)} %copy-done.10, ...), custom_call_target="tpu_custom_call" | custom-call | flops 10569646080 | bytes 3108864 | tf_op jit(solution)/shard_map/update_chunk/pallas_call | solution.py:93
  51.0 1.5 %collective-permute-start.1 = (bf16[2,8,69,256]{3,1,2,0:T(8,128)(2,1)S(1)}, bf16[2,8,69,256]{3,1,2,0:T(8,128)(2,1)S(1)}, u32[]{:S(2)}, u32[]{:S(2)}) collective-permute-start(bf16[2,8,69,256]{3,1,2,0:T(8,128)(2,1)S(1)} %copy.59), channel_id=1, source_target_pairs={{0,2},{1,3},{2,0},{3,1},{4,6},{5,7},{6,4},{7,5},{8,10},{9,11},{10,... | collective-permute-start | bytes 1695752 | tf_op jit(solution)/shard_map/ppermute | solution.py:190
  53.1 1.4 %slice_reduce_fusion = (f32[]{:T(128)}, f32[4,2]{1,0:T(4,128)S(1)}) fusion(f32[4,8,128]{2,1,0:T(8,128)} %get-tuple-element.7), kind=kLoop, calls=%fused_computation.23 | loop fusion | flops 2039 | bytes 4132 | tf_op jit(solution)/shard_map/reduce_sum | solution.py:220
  67.3 10.1 %collective-permute-done.1 = bf16[2,8,69,256]{3,1,2,0:T(8,128)(2,1)S(1)} collective-permute-done((bf16[2,8,69,256]{3,1,2,0:T(8,128)(2,1)S(1)}, bf16[2,8,69,256]{3,1,2,0:T(8,128)(2,1)S(1)}, u32[]{:S(2)}, u32[]{:S(2)}) %collective-permute-start.1) | collective-permute-done | bytes 565280 | tf_op jit(solution)/shard_map/ppermute | solution.py:190
  77.9 1.1 %fusion.9 = (bf16[1,8,69,256]{3,1,2,0:T(8,128)(2,1)S(1)}, bf16[1,8,69,256]{3,1,2,0:T(8,128)(2,1)S(1)}) fusion(bf16[2,8,69,256]{3,1,2,0:T(8,128)(2,1)} %collective-permute-done.3), kind=kLoop, calls=%fused_computation.45 | loop fusion | bytes 1130496 | tf_op jit(solution)/shard_map/slice | solution.py:196
  79.8 1.1 %fusion.11 = (bf16[1,8,69,256]{3,1,2,0:T(8,128)(2,1)S(1)}, bf16[1,8,69,256]{3,1,2,0:T(8,128)(2,1)S(1)}) fusion(bf16[2,8,69,256]{3,1,2,0:T(8,128)(2,1)} %collective-permute-done.5), kind=kLoop, calls=%fused_computation.47 | loop fusion | bytes 1130496 | tf_op jit(solution)/shard_map/slice | solution.py:196
  81.5 1.5 %copy_select_fusion.5 = (bf16[1,8,69,256]{3,2,1,0:T(8,128)(2,1)S(1)}, bf16[1,8,69,256]{3,2,1,0:T(8,128)(2,1)S(1)}) fusion(bf16[1,8,69,256]{3,1,2,0:T(8,128)(2,1)S(1)} %get-tuple-element.34, pred[]{:T(512)} %bitcast.8, pred[]{:T(512)} %bitcast.7, pred[]{:T(512)} %bitcast.1, pred[]{:T(512)} %bitcast, bf16[1,8,69,256]{3,1,2,0:T(8,128)(2,1)S(1)} %get-tuple-element.37, ...), kind=kLoop, calls=%fused_computation.13 | loop fusion | flops 1130496 | bytes 2261000 | tf_op jit(solution)/shard_map/jit(_where)/select_n | solution.py:201
  83.0 1.5 %copy_select_fusion.3 = (bf16[1,8,69,256]{3,2,1,0:T(8,128)(2,1)S(1)}, bf16[1,8,69,256]{3,2,1,0:T(8,128)(2,1)S(1)}) fusion(bf16[1,8,69,256]{3,1,2,0:T(8,128)(2,1)S(1)} %get-tuple-element.38, pred[]{:T(512)} %bitcast.8, pred[]{:T(512)} %bitcast.7, pred[]{:T(512)} %bitcast.1, pred[]{:T(512)} %bitcast, bf16[1,8,69,256]{3,1,2,0:T(8,128)(2,1)S(1)} %get-tuple-element.41, ...), kind=kLoop, calls=%fused_computation.11 | loop fusion | flops 1130496 | bytes 2261000 | tf_op jit(solution)/shard_map/jit(_where)/select_n | solution.py:201
  84.5 1.5 %copy_select_fusion.1 = (bf16[1,8,69,256]{3,2,1,0:T(8,128)(2,1)S(1)}, bf16[1,8,69,256]{3,2,1,0:T(8,128)(2,1)S(1)}) fusion(bf16[1,8,69,256]{3,1,2,0:T(8,128)(2,1)S(1)} %get-tuple-element.42, pred[]{:T(512)} %bitcast.8, pred[]{:T(512)} %bitcast.7, pred[]{:T(512)} %bitcast.1, pred[]{:T(512)} %bitcast, bf16[1,8,69,256]{3,1,2,0:T(8,128)(2,1)S(1)} %get-tuple-element.45, ...), kind=kLoop, calls=%fused_computation.9 | loop fusion | flops 1130496 | bytes 2261000 | tf_op jit(solution)/shard_map/jit(_where)/select_n | solution.py:201
  86.2 1.5 %copy.79 = bf16[2,69,24,256]{3,2,1,0:T(8,128)(2,1)} copy(bf16[2,69,24,256]{3,1,2,0:T(8,128)(2,1)S(1)} %maximum_bitcast_fusion) | data formatting | bytes 3391488
  (88 shorter events, 13.8 us)
Async XLA Ops:
  0.6 1.9 %copy-start.16 = (bf16[69,24,256]{2,1,0:T(8,128)(2,1)S(1)}, bf16[69,24,256]{2,1,0:T(8,128)(2,1)}, u32[]{:S(2)}) copy-start(bf16[69,24,256]{2,1,0:T(8,128)(2,1)} %param.10) | copy-start | bytes 2543620
  0.6 3.2 %copy-start.20 = (s32[24,256]{1,0:T(8,128)S(1)}, s32[24,256]{1,0:T(8,128)}, u32[]{:S(2)}) copy-start(s32[24,256]{1,0:T(8,128)} %param.12) | copy-start | bytes 73732
  0.7 3.2 %copy-start.19 = (f32[24,256]{1,0:T(8,128)S(1)}, f32[24,256]{1,0:T(8,128)}, u32[]{:S(2)}) copy-start(f32[24,256]{1,0:T(8,128)} %param.11) | copy-start | bytes 73732
  0.7 3.2 %copy-start.17 = (bf16[3,3,64,69]{3,2,1,0:T(8,128)(2,1)S(1)}, bf16[3,3,64,69]{3,2,1,0:T(8,128)(2,1)}, u32[]{:S(2)}) copy-start(bf16[3,3,64,69]{3,2,1,0:T(8,128)(2,1)} %param.15) | copy-start | bytes 238468
  0.7 57.9 %collective-permute-start = (s32[2]{0:T(128)}, s32[2]{0:T(128)S(1)}, u32[]{:S(2)}, u32[]{:S(2)}) collective-permute-start(s32[2]{0:T(128)} %param.13), channel_id=1, source_target_pairs={{0,1},{1,0},{2,3},{3,2},{4,5},{5,4},{6,7},{7,6},{8,9},{9,8},{10,11... | collective-permute-start | bytes 32 | tf_op jit(solution)/shard_map/ppermute | solution.py:211
  2.5 28.9 %copy-start.1 = (bf16[69,24,256]{2,0,1:T(8,128)(2,1)}, bf16[69,24,256]{2,0,1:T(8,128)(2,1)S(1)}, u32[]{:S(2)}) copy-start(bf16[69,24,256]{2,0,1:T(8,128)(2,1)S(1)} %copy.127) | copy-start | bytes 2543620
  2.5 1.7 %copy-start.18 = (bf16[3,3,69,64]{2,3,1,0:T(8,128)(2,1)S(1)}, bf16[3,3,69,64]{2,3,1,0:T(8,128)(2,1)}, u32[]{:S(2)}) copy-start(bf16[3,3,69,64]{2,3,1,0:T(8,128)(2,1)} %param.17) | copy-start | bytes 238468
  3.9 2.7 %copy-start.14 = (bf16[2,69,24,256]{3,2,1,0:T(8,128)(2,1)S(1)}, bf16[2,69,24,256]{3,2,1,0:T(8,128)(2,1)}, u32[]{:S(2)}) copy-start(bf16[2,69,24,256]{3,2,1,0:T(8,128)(2,1)} %param.9) | copy-start | bytes 5087236
  3.9 35.6 %copy-start.9 = (f32[24,1,256]{2,1,0:T(1,128)}, f32[24,1,256]{2,1,0:T(1,128)S(1)}, u32[]{:S(2)}) copy-start(f32[24,1,256]{2,1,0:T(1,128)S(1)} %broadcast_in_dim.2.ow_ref) | copy-start | bytes 73732
  4.3 35.3 %copy-start.5 = (bf16[192,240]{1,0:T(8,128)(2,1)}, bf16[192,240]{1,0:T(8,128)(2,1)S(1)}, u32[]{:S(2)}) copy-start(bf16[192,240]{1,0:T(8,128)(2,1)S(1)} %reshape.53.w1_ref) | copy-start | bytes 276484
  4.7 34.9 %copy-start.3 = (bf16[240,192]{1,0:T(8,128)(2,1)}, bf16[240,192]{1,0:T(8,128)(2,1)S(1)}, u32[]{:S(2)}) copy-start(bf16[240,192]{1,0:T(8,128)(2,1)S(1)} %reshape.58.w3_ref) | copy-start | bytes 276484
  6.6 1.8 %copy-start.13 = (f32[69,24,256]{2,1,0:T(8,128)S(1)}, f32[69,24,256]{2,1,0:T(8,128)}, u32[]{:S(2)}) copy-start(f32[69,24,256]{2,1,0:T(8,128)} %convert_element_type.17) | copy-start | bytes 5087236
  6.6 2.6 %copy-start.15 = (bf16[2,69,24,256]{3,2,1,0:T(8,128)(2,1)S(1)}, bf16[2,69,24,256]{3,2,1,0:T(8,128)(2,1)}, u32[]{:S(2)}) copy-start(bf16[2,69,24,256]{3,2,1,0:T(8,128)(2,1)} %param.9) | copy-start | bytes 5087236
  9.2 22.2 %copy-start = (bf16[2,69,24,256]{3,1,2,0:T(8,128)(2,1)S(1)}, bf16[2,69,24,256]{3,1,2,0:T(8,128)(2,1)}, u32[]{:S(2)}) copy-start(bf16[2,69,24,256]{3,1,2,0:T(8,128)(2,1)} %copy.126) | copy-start | bytes 5087236
  32.3 0.9 %copy-start.11 = (bf16[2,3,69,256]{3,2,1,0:T(8,128)(2,1)S(1)}, bf16[2,3,69,256]{3,2,1,0:T(8,128)(2,1)}, u32[]{:S(2)}) copy-start(bf16[2,3,69,256]{3,2,1,0:T(8,128)(2,1)} %get-tuple-element.5.low_ref) | copy-start | bytes 635908
  34.2 5.4 %copy-start.8 = (bf16[192,192]{1,0:T(8,128)(2,1)S(1)}, bf16[192,192]{1,0:T(8,128)(2,1)}, u32[]{:S(2)}) copy-start(bf16[192,192]{1,0:T(8,128)(2,1)} %reshape.54.w2_ref) | copy-start | bytes 221188
  38.1 41.7 %collective-permute-start.5 = (bf16[2,8,69,256]{3,1,2,0:T(8,128)(2,1)}, bf16[2,8,69,256]{3,1,2,0:T(8,128)(2,1)}, u32[]{:S(2)}, u32[]{:S(2)}) collective-permute-start(bf16[2,8,69,256]{3,1,2,0:T(8,128)(2,1)} %copy.73), channel_id=1, source_target_pairs={{0,2},{1,3},{2,0},{3,1},{4,6},{5,7},{6,4},{7,5},{8,10},{9,11},{10,... | collective-permute-start | bytes 1695752 | tf_op jit(solution)/shard_map/ppermute | solution.py:190
  39.6 1.2 %copy-start.2 = (bf16[69,24,256]{2,0,1:T(8,128)(2,1)S(1)}, bf16[69,24,256]{2,0,1:T(8,128)(2,1)}, u32[]{:S(2)}) copy-start(bf16[69,24,256]{2,0,1:T(8,128)(2,1)} %copy-done.1) | copy-start | bytes 2543620
  44.7 33.1 %collective-permute-start.3 = (bf16[2,8,69,256]{3,1,2,0:T(8,128)(2,1)}, bf16[2,8,69,256]{3,1,2,0:T(8,128)(2,1)}, u32[]{:S(2)}, u32[]{:S(2)}) collective-permute-start(bf16[2,8,69,256]{3,1,2,0:T(8,128)(2,1)} %copy.66), channel_id=1, source_target_pairs={{0,2},{1,3},{2,0},{3,1},{4,6},{5,7},{6,4},{7,5},{8,10},{9,11},{10,... | collective-permute-start | bytes 1695752 | tf_op jit(solution)/shard_map/ppermute | solution.py:190
  47.9 10.7 %copy-start.21 = (s32[2]{0:T(128)S(1)}, s32[2]{0:T(128)}, u32[]{:S(2)}) copy-start(s32[2]{0:T(128)} %param.13) | copy-start | bytes 28
  51.0 26.4 %collective-permute-start.1 = (bf16[2,8,69,256]{3,1,2,0:T(8,128)(2,1)S(1)}, bf16[2,8,69,256]{3,1,2,0:T(8,128)(2,1)S(1)}, u32[]{:S(2)}, u32[]{:S(2)}) collective-permute-start(bf16[2,8,69,256]{3,1,2,0:T(8,128)(2,1)S(1)} %copy.59), channel_id=1, source_target_pairs={{0,2},{1,3},{2,0},{3,1},{4,6},{5,7},{6,4},{7,5},{8,10},{9,11},{10,... | collective-permute-start | bytes 1695752 | tf_op jit(solution)/shard_map/ppermute | solution.py:190
  77.8 3.6 %collective-permute-start.2 = (bf16[2,8,69,256]{3,1,2,0:T(8,128)(2,1)S(1)}, bf16[2,8,69,256]{3,1,2,0:T(8,128)(2,1)S(1)}, u32[]{:S(2)}, u32[]{:S(2)}) collective-permute-start(bf16[2,8,69,256]{3,1,2,0:T(8,128)(2,1)S(1)} %copy.62), channel_id=1, source_target_pairs={{0,1},{1,0},{2,3},{3,2},{4,5},{5,4},{6,7},{7,6},{8,9},{9,8},{10,11... | collective-permute-start | bytes 1695752 | tf_op jit(solution)/shard_map/ppermute | solution.py:200
  79.3 2.1 %collective-permute-start.4 = (bf16[2,8,69,256]{3,1,2,0:T(8,128)(2,1)S(1)}, bf16[2,8,69,256]{3,1,2,0:T(8,128)(2,1)S(1)}, u32[]{:S(2)}, u32[]{:S(2)}) collective-permute-start(bf16[2,8,69,256]{3,1,2,0:T(8,128)(2,1)S(1)} %copy.69), channel_id=1, source_target_pairs={{0,1},{1,0},{2,3},{3,2},{4,5},{5,4},{6,7},{7,6},{8,9},{9,8},{10,11... | collective-permute-start | bytes 1695752 | tf_op jit(solution)/shard_map/ppermute | solution.py:200
  81.3 3.2 %collective-permute-start.6 = (bf16[2,8,69,256]{3,1,2,0:T(8,128)(2,1)S(1)}, bf16[2,8,69,256]{3,1,2,0:T(8,128)(2,1)S(1)}, u32[]{:S(2)}, u32[]{:S(2)}) collective-permute-start(bf16[2,8,69,256]{3,1,2,0:T(8,128)(2,1)S(1)} %copy.76), channel_id=1, source_target_pairs={{0,1},{1,0},{2,3},{3,2},{4,5},{5,4},{6,7},{7,6},{8,9},{9,8},{10,11... | collective-permute-start | bytes 1695752 | tf_op jit(solution)/shard_map/ppermute | solution.py:200
  (5 other events, 4.4 us)

commit v3 on v2

v3 whole, which is shorter than its diff:
```python
import functools

import jax
import jax.numpy as jnp
from jax import lax
from jax.experimental import pallas as pl
from jax.experimental.pallas import tpu as pltpu
from jax.sharding import PartitionSpec as P


def pad_to(count, step):
    return -(-count // step) * step


def stacked_taps(weight, out_rows, in_rows):
    _, _, outs, ins = weight.shape
    w = jnp.pad(weight, ((0, 0), (0, 0), (0, out_rows - outs), (0, in_rows - ins)))
    return w.transpose(1, 2, 0, 3).reshape(3 * out_rows, 3 * in_rows)


def conv_column(src_ref, w, x, in_rows, out_rows, first, last):
    window = src_ref[x * in_rows : (x + 3) * in_rows, :]
    p = jnp.dot(w, window, preferred_element_type=jnp.float32)
    lat = p.shape[1]
    below = pltpu.roll(p[:out_rows], 1, 1)
    above = pltpu.roll(p[2 * out_rows :], lat - 1, 1)
    return (
        p[out_rows : 2 * out_rows]
        + jnp.where(first, 0.0, below)
        + jnp.where(last, 0.0, above)
    )


def silu(v):
    half = 0.5 * v
    return half + half * jnp.tanh(half)


def step_kernel(spans, cin, hid, edges, *refs):
    if edges:
        low_ref, high_ref, *refs = refs
    mid_ref, obs_ref, ow_ref, w1_ref, w2_ref, w3_ref, out_ref, ext, a1, a2 = refs
    cols, nvars, lat = mid_ref.shape[1:]
    lane_h = lax.broadcasted_iota(jnp.int32, (hid, lat), 1)
    lane_o = lax.broadcasted_iota(jnp.int32, (cin, lat), 1)
    first_h, last_h = lane_h == 0, lane_h == lat - 1
    first_o, last_o = lane_o == 0, lane_o == lat - 1

    @pl.when(pl.program_id(0) == 0)
    def _():
        ext[...] = jnp.zeros_like(ext)

    at = 0
    for s, (lo, hi) in enumerate(spans):
        for k, x in enumerate(range(lo - 3, hi + 3)):
            if x < 0:
                column = low_ref[0, x + 3]
            elif x >= cols:
                column = high_ref[0, x - cols]
            else:
                column = mid_ref[0, x]
            ext[s, k * cin : k * cin + nvars, :] = column
        for x in range(hi - lo + 4):
            v = conv_column(ext.at[s], w1_ref[...], x, cin, hid, first_h, last_h)
            a1[s, x * hid : (x + 1) * hid, :] = silu(v).astype(jnp.bfloat16)
        for x in range(hi - lo + 2):
            v = conv_column(a1.at[s], w2_ref[...], x, hid, hid, first_h, last_h)
            a2[s, x * hid : (x + 1) * hid, :] = silu(v).astype(jnp.bfloat16)
        for x in range(hi - lo):
            noise = conv_column(a2.at[s], w3_ref[...], x, hid, cin, first_o, last_o)[:nvars]
            current = ext[s, (x + 3) * cin : (x + 4) * cin, :].astype(jnp.float32)[:nvars]
            seen = obs_ref[lo + x].astype(jnp.float32)
            gain = 0.25 * ow_ref[lo + x]
            new = current - 0.5 * noise + gain * (seen - current)
            out_ref[0, at] = new.astype(jnp.bfloat16)
            at += 1


def update_chunk(spans, edges, mid, observed, obs_weight, w1, w2, w3, cin, hid):
    slots, _, nvars, lat = mid.shape
    step = sum(hi - lo for lo, hi in spans)
    widest = max(hi - lo for lo, hi in spans)
    whole = lambda a: pl.BlockSpec(a.shape, lambda p: (0,) * a.ndim)
    own = lambda a: pl.BlockSpec((1,) + a.shape[1:], lambda p: (p, 0, 0, 0))
    return pl.pallas_call(
        functools.partial(step_kernel, spans, cin, hid, bool(edges)),
        out_shape=jax.ShapeDtypeStruct((slots, step, nvars, lat), jnp.bfloat16),
        grid=(slots,),
        in_specs=[own(a) for a in (*edges, mid)]
        + [whole(a) for a in (observed, obs_weight, w1, w2, w3)],
        out_specs=pl.BlockSpec((1, step, nvars, lat), lambda p: (p, 0, 0, 0)),
        scratch_shapes=[
            pltpu.VMEM((len(spans), (widest + 6) * cin, lat), jnp.bfloat16),
            pltpu.VMEM((len(spans), (widest + 4) * hid, lat), jnp.bfloat16),
            pltpu.VMEM((len(spans), (widest + 2) * hid, lat), jnp.bfloat16),
        ],
        compiler_params=pltpu.CompilerParams(vmem_limit_bytes=24 << 20),
        cost_estimate=pl.CostEstimate(flops=0, bytes_accessed=1024, transcendentals=0),
        name="update_chunk",
    )(*edges, mid, observed, obs_weight, w1, w2, w3)


def exchange_kernel(n_lon, mid_ref, sums_ref, low_ref, high_ref, total_ref, parts, edge_send, edge_recv, lon_send, lon_recv):
    lon = lax.axis_index("lon")
    cols = mid_ref.shape[1]

    def lon_at(k):
        return {"lon": lax.rem(lon + k, n_lon)}

    barrier = pltpu.get_barrier_semaphore()
    for k in range(1, n_lon):
        pl.semaphore_signal(barrier, inc=1, device_id=lon_at(k), device_id_type=pl.DeviceIdType.MESH)
    pl.semaphore_wait(barrier, n_lon - 1)

    def send(src, dst, s, r, target):
        copy = pltpu.make_async_remote_copy(
            src_ref=src, dst_ref=dst, send_sem=s, recv_sem=r,
            device_id=target, device_id_type=pl.DeviceIdType.MESH,
        )
        copy.start()
        return copy

    edges = [
        send(mid_ref.at[:, cols - 3 : cols], low_ref, edge_send.at[0], edge_recv.at[0], lon_at(1)),
        send(mid_ref.at[:, 0:3], high_ref, edge_send.at[1], edge_recv.at[1], lon_at(n_lon - 1)),
    ]
    parts[lon] = sums_ref[...]
    over_lon = [
        send(sums_ref, parts.at[lon], lon_send.at[k - 1], lon_recv.at[k - 1], lon_at(k))
        for k in range(1, n_lon)
    ]
    for copy in over_lon:
        copy.wait()
    band_sum = parts[0]
    for k in range(1, n_lon):
        band_sum = band_sum + parts[k]
    total_ref[...] = band_sum
    for copy in edges:
        copy.wait()


def exchange(mid, sums, n_lon):
    slots, _, nvars, lat = mid.shape
    edge = jax.ShapeDtypeStruct((slots, 3, nvars, lat), mid.dtype)
    vmem = pl.BlockSpec(memory_space=pltpu.VMEM)
    return pl.pallas_call(
        functools.partial(exchange_kernel, n_lon),
        out_shape=(edge, edge, jax.ShapeDtypeStruct(sums.shape, jnp.float32)),
        in_specs=[pl.BlockSpec(memory_space=pl.ANY), vmem],
        out_specs=(vmem, vmem, vmem),
        scratch_shapes=[
            pltpu.VMEM((n_lon,) + sums.shape, jnp.float32),
            pltpu.SemaphoreType.DMA((2,)),
            pltpu.SemaphoreType.DMA((2,)),
            pltpu.SemaphoreType.DMA((n_lon - 1,)),
            pltpu.SemaphoreType.DMA((n_lon - 1,)),
        ],
        compiler_params=pltpu.CompilerParams(collective_id=0, has_side_effects=True),
        cost_estimate=pl.CostEstimate(flops=0, bytes_accessed=1024, transcendentals=0),
        name="exchange",
    )(mid, sums)


def across(u):
    n = lax.axis_size("dom")
    return [u] + [
        lax.ppermute(u, "dom", [(d, (d + 2 * k) % n) for d in range(n)]) for k in range(1, n // 2)
    ]


def pick(pieces, c):
    slots = pieces[0].shape[0]
    value = pieces[0][0]
    for m in range(1, len(pieces) * slots):
        value = jnp.where(c == m, pieces[m // slots][m % slots], value)
    return value


def on_device(particles, observed, precision, stations, ancestors, tempering, w_in, w_mid, w_out):
    slots, nvars, cols, lat = particles.shape
    hid = w_mid.shape[2]
    cin = pad_to(nvars, 16)
    n_dom, n_lon = lax.axis_size("dom"), lax.axis_size("lon")
    me = lax.axis_index("dom")
    mid = particles.transpose(0, 2, 1, 3)
    sibling_anc = lax.ppermute(ancestors, "dom", [(d, d ^ 1) for d in range(n_dom)])

    obs_weight = stations.astype(jnp.float32) * precision
    wanted = jnp.concatenate([ancestors, sibling_anc])
    owner = lax.div(wanted, slots)
    chips = n_dom // 2
    steps = lax.rem(lax.shift_right_logical(me, 1) - lax.div(owner, 2) + chips, chips)
    candidate = steps * slots + lax.rem(wanted, slots)
    here = lax.rem(owner, 2) == (me & 1)

    obs_columns = observed.transpose(1, 0, 2)
    ow_columns = obs_weight[:, None, :]
    w1 = stacked_taps(w_in, hid, cin)
    w2 = stacked_taps(w_mid, hid, hid)
    w3 = stacked_taps(w_out, cin, hid)

    update = lambda spans, edges: update_chunk(
        spans, edges, mid, obs_columns, ow_columns, w1, w2, w3, cin, hid
    )
    u = update([(3, cols - 3)], [])
    groups = [across(u)]

    late_weight, _ = lax.optimization_barrier((obs_weight, u))
    misfit_cell = particles.astype(jnp.float32) - observed.astype(jnp.float32)[None]
    local_sums = jnp.sum(late_weight[None, None] * misfit_cell * misfit_cell, axis=(1, 2))
    sums = jnp.sum(local_sums.reshape(slots, lat // 128, 128), axis=1)
    sums = jnp.pad(sums, ((0, pad_to(slots, 8) - slots), (0, 0)))
    low, high, band_sums = exchange(mid, sums, n_lon)
    groups.append(across(update([(0, 3), (cols - 3, cols)], [low, high])))

    own_misfit = jnp.sum(band_sums[:slots], axis=1)
    every_sum = jnp.concatenate(
        [own_misfit]
        + [
            lax.ppermute(own_misfit, "dom", [(d, (d + k) % n_dom) for d in range(n_dom)])
            for k in range(1, n_dom)
        ]
    )
    center = jnp.mean(every_sum)
    deviation = every_sum - center
    spread = jnp.sqrt(jnp.mean(deviation * deviation) + 1.0)
    expo = jnp.exp(-0.5 * tempering[0] * deviation / spread)
    own_weights = expo[:slots] / jnp.sum(expo)

    done, before = [], None
    for pieces in groups:
        if before is not None:
            *pieces, before = lax.optimization_barrier((*pieces, before))
            done[-1] = before
        sent = jnp.stack([pick(pieces, candidate[slots + s]) for s in range(slots)])
        before = sent
        done.append(sent)
        groups[len(done) - 1] = pieces
    results = []
    for pieces, sent in zip(groups, done):
        received = lax.ppermute(sent, "dom", [(d, d ^ 1) for d in range(n_dom)])
        results.append(
            jnp.stack([jnp.where(here[s], pick(pieces, candidate[s]), received[s]) for s in range(slots)])
        )
    inner, sides = results
    new_columns = jnp.concatenate([sides[:, :3], inner, sides[:, 3:]], axis=1)
    return (new_columns.transpose(0, 2, 1, 3), own_weights)


def solution(mesh):
    return jax.shard_map(
        on_device,
        mesh=mesh,
        in_specs=(
            P(("ens", "dom"), None, "lon", None),
            P("ens", "lon", None),
            P(("ens", "lon"), None),
            P(("ens", "lon"), None),
            P(("ens", "dom")),
            P("ens"),
            P(),
            P(),
            P(),
        ),
        out_specs=(P(("ens", "dom"), None, "lon", None), P(("ens", "dom"))),
        check_vma=False,
    )
```

time: 88.4 us -> 81.5 us (0.922)
  waiting for transfers between devices: 10.1 us -> 0.5 us
  Pallas kernels: 30.1 us -> 24.9 us
  starting transfers between devices: 4.73 us -> 7.14 us
  local copies, waits for them, and re-layouts: 21.8 us -> 23.7 us
  between operations: 10.3 us -> 12.2 us
  other arithmetic: 10.7 us -> 12.3 us
    ppermute x6 -> x7, waiting for transfers between devices: 10.1 us -> 0.5 us  [the longest x2 0.48 us: on_device(): received = lax.ppermute(sent, 'dom', [(d, d ^ 1) for d in range(n_dom)])]
    pallas_call x4 -> x3, Pallas kernels: 30.1 us -> 24.9 us  [the longest x1 15.8 us: exchange(): pl.pallas_call(functools.partial(exchange_kernel, n_lon), out_shape=(edge...]
    reduce_sum x1 -> x4, other arithmetic: 1.4 us -> 4.45 us  [on_device(): center = jnp.mean(every_sum)]
    ppermute x6 -> x7, starting transfers between devices: 4.21 us -> 7.14 us  [the longest x2 3.55 us: across(): lax.ppermute(u, 'dom', [(d, (d + 2 * k) % n) for d in range(n)])]
    slice x3 -> x1, local copies, waits for them, and re-layouts: 2.2 us -> 3.89 us  [pick(): value = jnp.where(c == m, pieces[m // slots][m % slots], value)]
    select_n x3 -> x2, other arithmetic: 4.46 us -> 2.86 us  [on_device(): jnp.where(here[s], pick(pieces, candidate[s]), received[s])]
    slice x5 -> x3, local copies, waits for them, and re-layouts: 1.44 us -> 2.93 us  [the longest x1 1.76 us: on_device(): received[s]]
    convert_element_type x1, other arithmetic: 1.31 us -> 0.12 us  [on_device(): observed.astype(jnp.float32)[None]]
  transfers between devices with their start and end apart: 7 -> 8, of which waited for: 1 -> 1; matrix products, arithmetic and copies ran while one was open for 25% -> 20% of each run, Pallas kernels for 34% -> 24%
where the time goes in v3:
time: 81.5 us; the launch traced here: 80.8 us
  Pallas kernels  24.9 us (31%)
  local copies, waits for them, and re-layouts  23.7 us (29%)
  other arithmetic  12.3 us (15%)
  between operations  12.2 us (15%)
  starting transfers between devices  7.14 us (9%)
    pallas_call x1, Pallas kernels, exchange(): pl.pallas_call(functools.partial(exchange_kernel, n_lon), out_shape=(edge...  15.8 us
    unnamed x49, local copies, waits for them, and re-layouts  12.2 us
    pallas_call x2, Pallas kernels, update_chunk(): pl.pallas_call(functools.partial(step_kernel, spans, cin, hid, bool(edges...  9.11 us
    reduce_sum x4, other arithmetic, on_device(): center = jnp.mean(every_sum)  4.45 us
    slice x1, local copies, waits for them, and re-layouts, pick(): value = jnp.where(c == m, pieces[m // slots][m % slots], value)  3.89 us
    ppermute x2, starting transfers between devices, across(): lax.ppermute(u, 'dom', [(d, (d + 2 * k) % n) for d in range(n)])  3.55 us
    ppermute x3, starting transfers between devices, on_device(): lax.ppermute(own_misfit, 'dom', [(d, (d + k) % n_dom) for d in range(n_do...  2.95 us
    select_n x2, other arithmetic, on_device(): jnp.where(here[s], pick(pieces, candidate[s]), received[s])  2.86 us
  transfers between devices with their start and end apart: 8, of which 1 were waited for; matrix products, arithmetic and copies ran while one was open for 20% of the time, Pallas kernels for 24%

profile of v3, /device:TPU:0, one launch (start us, length us, event | category | flops | bytes accessed | tf_op | source)
XLA Modules:
  0.0 80.8 jit_solution(862768002938210194)
XLA Ops:
  0.6 1.9 %copy.65 = bf16[2,69,24,256]{3,1,2,0:T(8,128)(2,1)S(1)} copy(bf16[2,69,24,256]{3,2,1,0:T(8,128)(2,1)} %param.9) | data formatting | bytes 3391488 | tf_op args[0]
  2.6 1.1 %copy.66 = bf16[69,24,256]{2,0,1:T(8,128)(2,1)} copy(bf16[69,24,256]{2,1,0:T(8,128)(2,1)S(1)} %copy-done.15) | data formatting | bytes 1695744 | tf_op args[1]
  4.9 1.2 %copy-done.2 = bf16[69,24,256]{2,0,1:T(8,128)(2,1)S(1)} copy-done((bf16[69,24,256]{2,0,1:T(8,128)(2,1)S(1)}, bf16[69,24,256]{2,0,1:T(8,128)(2,1)}, u32[]{:S(2)}) %copy-start.2) | copy-done | bytes 847896
  6.1 5.3 %update_chunk.2 = bf16[2,18,69,256]{3,2,1,0:T(8,128)(2,1)S(1)} custom-call(bf16[2,24,69,256]{3,2,1,0:T(8,128)(2,1)S(1)} %bitcast.28, bf16[24,69,256]{2,1,0:T(8,128)(2,1)S(1)} %bitcast.31, f32[24,1,256]{2,1,0:T(1,128)S(1)} %broadcast_in_dim.2.refs_2_.refs_4_, bf16[192,240]{1,0:T(8,128)(2,1)S(1)} %reshape.44.refs_3_.refs_5_, ...), custom_call_target="tpu_custom_call" | custom-call | bytes 1024 | tf_op jit(solution)/shard_map/update_chunk/pallas_call | solution.py:85
  11.4 2.0 %copy.46 = bf16[2,18,69,256]{3,0,2,1:T(2,128)(2,1)} copy(bf16[2,18,69,256]{3,2,1,0:T(8,128)(2,1)S(1)} %update_chunk.2) | data formatting | bytes 2543616 | tf_op jit(solution)/shard_map/update_chunk/pallas_call | solution.py:85
  13.5 2.9 %collective-permute-start.2 = (bf16[2,18,69,256]{3,0,2,1:T(2,128)(2,1)}, bf16[2,18,69,256]{3,0,2,1:T(2,128)(2,1)}, u32[]{:S(2)}, u32[]{:S(2)}) collective-permute-start(bf16[2,18,69,256]{3,0,2,1:T(2,128)(2,1)} %copy.46), channel_id=1, source_target_pairs={{0,2},{1,3},{2,0},{3,1},{4,6},{5,7},{6,4},{7,5},{8,10},{9,11},{10,... | collective-permute-start | bytes 3815432 | tf_op jit(solution)/shard_map/ppermute | solution.py:167
  17.8 15.8 %exchange.1 = (bf16[2,3,69,256]{3,2,1,0:T(8,128)(2,1)}, bf16[2,3,69,256]{3,2,1,0:T(8,128)(2,1)}, f32[8,128]{1,0:T(8,128)}) custom-call(bf16[2,24,69,256]{3,2,1,0:T(8,128)(2,1)} %bitcast.29, f32[8,128]{1,0:T(8,128)} %pad.14.sums_ref), custom_call_target="tpu_custom_call" | custom-call | bytes 1024 | tf_op jit(solution)/shard_map/exchange/pallas_call | solution.py:146
  33.6 1.3 %slice_reduce_fusion = (f32[]{:T(128)}, f32[2]{0:T(128)S(1)}) fusion(f32[8,128]{1,0:T(8,128)} %get-tuple-element.15), kind=kLoop, calls=%fused_computation.34 | loop fusion | flops 509 | bytes 1036 | tf_op jit(solution)/shard_map/reduce_sum | solution.py:224
  34.9 1.5 %collective-permute-start.6 = (f32[2]{0:T(128)S(1)}, f32[2]{0:T(128)}, u32[]{:S(2)}, u32[]{:S(2)}) collective-permute-start(f32[2]{0:T(128)S(1)} %get-tuple-element.25), channel_id=1, source_target_pairs={{0,2},{1,3},{2,0},{3,1},{4,6},{5,7},{6,4},{7,5},{8,10},{9,11},{10,... | collective-permute-start | bytes 32 | tf_op jit(solution)/shard_map/ppermute | solution.py:220
  36.4 1.4 %collective-permute-start.7 = (f32[2]{0:T(128)S(1)}, f32[2]{0:T(128)}, u32[]{:S(2)}, u32[]{:S(2)}) collective-permute-start(f32[2]{0:T(128)S(1)} %get-tuple-element.25), channel_id=1, source_target_pairs={{0,3},{1,0},{2,1},{3,2},{4,7},{5,4},{6,5},{7,6},{8,11},{9,8},{10,9... | collective-permute-start | bytes 32 | tf_op jit(solution)/shard_map/ppermute | solution.py:220
  38.5 1.2 %copy-done.3 = bf16[69,24,256]{2,0,1:T(8,128)(2,1)S(1)} copy-done((bf16[69,24,256]{2,0,1:T(8,128)(2,1)S(1)}, bf16[69,24,256]{2,0,1:T(8,128)(2,1)}, u32[]{:S(2)}) %copy-start.3) | copy-done | bytes 847896
  43.1 0.9 %copy-done.12 = bf16[2,3,69,256]{3,2,1,0:T(8,128)(2,1)S(1)} copy-done((bf16[2,3,69,256]{3,2,1,0:T(8,128)(2,1)S(1)}, bf16[2,3,69,256]{3,2,1,0:T(8,128)(2,1)}, u32[]{:S(2)}) %copy-start.12) | copy-done | bytes 211992
  44.1 0.9 %copy-done.13 = bf16[2,3,69,256]{3,2,1,0:T(8,128)(2,1)S(1)} copy-done((bf16[2,3,69,256]{3,2,1,0:T(8,128)(2,1)S(1)}, bf16[2,3,69,256]{3,2,1,0:T(8,128)(2,1)}, u32[]{:S(2)}) %copy-start.13) | copy-done | bytes 211992
  45.0 3.8 %update_chunk.3 = bf16[2,6,69,256]{3,2,1,0:T(8,128)(2,1)S(1)} custom-call(bf16[2,3,69,256]{3,2,1,0:T(8,128)(2,1)S(1)} %copy-done.12, bf16[2,3,69,256]{3,2,1,0:T(8,128)(2,1)S(1)} %copy-done.13, bf16[2,24,69,256]{3,2,1,0:T(8,128)(2,1)S(1)} %bitcast.30, bf16[24,69,256]{2,1,0:T(8,128)(2,1)S(1)} %bitcast.32, f32[24,1,256]{2,1,0:T(1,128)S(1)} %copy-done.11, ...), custom_call_target="tpu_custom_call" | custom-call | bytes 1024 | tf_op jit(solution)/shard_map/update_chunk/pallas_call | solution.py:85
  59.3 1.3 %reduce_sum.84 = f32[]{:T(128)} reduce(f32[2]{0:T(128)} %collective-permute-done.6, f32[]{:T(128)} %constant.45.clone.1), dimensions={0}, to_apply=%region_5.6 | reduce | flops 1 | bytes 16 | tf_op jit(solution)/shard_map/reduce_sum | solution.py:224
  61.3 1.3 %reduce_sum.86 = f32[]{:T(128)} reduce(f32[2]{0:T(128)} %collective-permute-done.7, f32[]{:T(128)} %constant.45.clone.1), dimensions={0}, to_apply=%region_6.7 | reduce | flops 1 | bytes 16 | tf_op jit(solution)/shard_map/reduce_sum | solution.py:224
  63.2 1.4 %multiply_reduce_fusion = (f32[]{:T(128)}, f32[8]{0:T(128)S(1)}) fusion(f32[]{:T(128)S(6)} %div.50, f32[2]{0:T(128)} %collective-permute-done.7, f32[2]{0:T(128)} %collective-permute-done.6, f32[2]{0:T(128)S(1)} %collective-permute-done.5, f32[2]{0:T(128)S(1)} %get-tuple-element.25), kind=kLoop, calls=%fused_computation.43 | loop fusion | flops 47 | bytes 72 | tf_op jit(solution)/shard_map/reduce_sum | solution.py:226
  65.2 3.9 %fusion.13 = (bf16[1,18,69,256]{3,0,2,1:T(2,128)(2,1)S(1)}, bf16[1,18,69,256]{3,0,2,1:T(2,128)(2,1)S(1)}) fusion(bf16[2,18,69,256]{3,0,2,1:T(2,128)(2,1)} %collective-permute-done.2), kind=kLoop, calls=%fused_computation.47 | loop fusion | bytes 2543616 | tf_op jit(solution)/shard_map/slice | solution.py:175
  69.7 1.0 %copy.49 = bf16[2,18,69,256]{3,0,2,1:T(2,128)(2,1)S(1)} copy(bf16[2,18,69,256]{3,2,1,0:T(8,128)(2,1)S(1)} %pad_maximum_fusion) | data formatting | bytes 2543616 | tf_op jit(solution)/shard_map/optimization_barrier | solution.py:233
  72.7 1.2 %slice_divide_fusion = f32[2]{0:T(128)} fusion(f32[8]{0:T(128)S(1)} %get-tuple-element.27, f32[]{:T(128)} %get-tuple-element.26), kind=kLoop, calls=%fused_computation.41 | loop fusion | flops 2 | bytes 20 | tf_op jit(solution)/shard_map/div | solution.py:228
  74.4 1.3 %slice_select_fusion.1 = (bf16[1,6,69,256]{3,2,1,0:T(8,128)(2,1)S(1)}, bf16[1,6,69,256]{3,2,1,0:T(8,128)(2,1)S(1)}) fusion(bf16[2,6,69,256]{3,2,1,0:T(8,128)(2,1)S(1)} %collective-permute-done.3, pred[]{:T(512)} %bitcast.14, pred[]{:T(512)} %bitcast.13, pred[]{:T(512)} %bitcast.1, pred[]{:T(512)} %bitcast, bf16[2,6,69,256]{3,2,1,0:T(8,128)(2,1)S(1)} %update_chunk.3, ...), kind=kLoop, calls=%fused_computation.20 | loop fusion | flops 847872 | bytes 1695752 | tf_op jit(solution)/shard_map/jit(_where)/select_n | solution.py:243
  75.7 1.8 %fusion.12 = (bf16[1,18,69,256]{3,0,2,1:T(2,128)(2,1)S(1)}, bf16[1,18,69,256]{3,0,2,1:T(2,128)(2,1)S(1)}) fusion(bf16[2,18,69,256]{3,0,2,1:T(2,128)(2,1)S(1)} %collective-permute-done.4), kind=kLoop, calls=%fused_computation.46 | loop fusion | bytes 2543616 | tf_op jit(solution)/shard_map/slice | solution.py:243
  77.5 1.6 %copy_select_fusion.1 = (bf16[1,18,69,256]{3,2,1,0:T(8,128)(2,1)S(1)}, bf16[1,18,69,256]{3,2,1,0:T(8,128)(2,1)S(1)}) fusion(bf16[1,18,69,256]{3,0,2,1:T(2,128)(2,1)S(1)} %get-tuple-element.39, bf16[1,18,69,256]{3,2,1,0:T(8,128)(2,1)S(1)} %get-tuple-element.34, bf16[1,18,69,256]{3,2,1,0:T(8,128)(2,1)S(1)} %get-tuple-element.33, pred[]{:T(512)} %bitcast.14, ...), kind=kLoop, calls=%fused_computation.12 | loop fusion | flops 2543616 | bytes 5087240 | tf_op jit(solution)/shard_map/jit(_where)/select_n | solution.py:243
  79.2 1.5 %copy.52 = bf16[2,69,24,256]{3,2,1,0:T(8,128)(2,1)} copy(bf16[2,69,24,256]{3,1,2,0:T(8,128)(2,1)S(1)} %fusion.5) | data formatting | bytes 3391488
  (83 shorter events, 11.1 us)
Async XLA Ops:
  0.6 1.9 %copy-start.15 = (bf16[69,24,256]{2,1,0:T(8,128)(2,1)S(1)}, bf16[69,24,256]{2,1,0:T(8,128)(2,1)}, u32[]{:S(2)}) copy-start(bf16[69,24,256]{2,1,0:T(8,128)(2,1)} %param.10) | copy-start | bytes 2543620
  2.5 2.3 %copy-start = (bf16[2,69,24,256]{3,1,2,0:T(8,128)(2,1)}, bf16[2,69,24,256]{3,1,2,0:T(8,128)(2,1)S(1)}, u32[]{:S(2)}) copy-start(bf16[2,69,24,256]{3,1,2,0:T(8,128)(2,1)S(1)} %copy.65) | copy-start | bytes 5087236
  2.5 1.2 %copy-start.20 = (f32[24,256]{1,0:T(8,128)S(1)}, f32[24,256]{1,0:T(8,128)}, u32[]{:S(2)}) copy-start(f32[24,256]{1,0:T(8,128)} %param.11) | copy-start | bytes 73732
  2.6 1.2 %copy-start.17 = (bf16[3,3,64,69]{3,2,1,0:T(8,128)(2,1)S(1)}, bf16[3,3,64,69]{3,2,1,0:T(8,128)(2,1)}, u32[]{:S(2)}) copy-start(bf16[3,3,64,69]{3,2,1,0:T(8,128)(2,1)} %param.15) | copy-start | bytes 238468
  2.6 1.5 %copy-start.19 = (bf16[3,3,64,64]{3,2,1,0:T(8,128)(2,1)S(1)}, bf16[3,3,64,64]{3,2,1,0:T(8,128)(2,1)}, u32[]{:S(2)}) copy-start(bf16[3,3,64,64]{3,2,1,0:T(8,128)(2,1)} %param.16) | copy-start | bytes 221188
  2.6 1.8 %copy-start.18 = (bf16[3,3,69,64]{2,3,1,0:T(8,128)(2,1)S(1)}, bf16[3,3,69,64]{2,3,1,0:T(8,128)(2,1)}, u32[]{:S(2)}) copy-start(bf16[3,3,69,64]{2,3,1,0:T(8,128)(2,1)} %param.17) | copy-start | bytes 238468
  3.8 7.6 %copy-start.10 = (f32[24,1,256]{2,1,0:T(1,128)}, f32[24,1,256]{2,1,0:T(1,128)S(1)}, u32[]{:S(2)}) copy-start(f32[24,1,256]{2,1,0:T(1,128)S(1)} %broadcast_in_dim.2.refs_2_.refs_4_) | copy-start | bytes 73732
  4.1 7.3 %copy-start.6 = (bf16[192,240]{1,0:T(8,128)(2,1)}, bf16[192,240]{1,0:T(8,128)(2,1)S(1)}, u32[]{:S(2)}) copy-start(bf16[192,240]{1,0:T(8,128)(2,1)S(1)} %reshape.44.refs_3_.refs_5_) | copy-start | bytes 276484
  4.4 7.0 %copy-start.8 = (bf16[192,192]{1,0:T(8,128)(2,1)}, bf16[192,192]{1,0:T(8,128)(2,1)S(1)}, u32[]{:S(2)}) copy-start(bf16[192,192]{1,0:T(8,128)(2,1)S(1)} %reshape.45.refs_4_.refs_6_) | copy-start | bytes 221188
  4.8 6.6 %copy-start.4 = (bf16[240,192]{1,0:T(8,128)(2,1)}, bf16[240,192]{1,0:T(8,128)(2,1)S(1)}, u32[]{:S(2)}) copy-start(bf16[240,192]{1,0:T(8,128)(2,1)S(1)} %reshape.48.refs_5_.refs_7_) | copy-start | bytes 276484
  4.9 1.2 %copy-start.2 = (bf16[69,24,256]{2,0,1:T(8,128)(2,1)S(1)}, bf16[69,24,256]{2,0,1:T(8,128)(2,1)}, u32[]{:S(2)}) copy-start(bf16[69,24,256]{2,0,1:T(8,128)(2,1)} %copy.66) | copy-start | bytes 2543620
  11.4 5.0 %copy-start.16 = (bf16[69,24,256]{2,1,0:T(8,128)(2,1)S(1)}, bf16[69,24,256]{2,1,0:T(8,128)(2,1)}, u32[]{:S(2)}) copy-start(bf16[69,24,256]{2,1,0:T(8,128)(2,1)} %param.10) | copy-start | bytes 2543620
  13.5 3.1 %copy-start.14 = (bf16[2,69,24,256]{3,2,1,0:T(8,128)(2,1)S(1)}, bf16[2,69,24,256]{3,2,1,0:T(8,128)(2,1)}, u32[]{:S(2)}) copy-start(bf16[2,69,24,256]{3,2,1,0:T(8,128)(2,1)} %param.9) | copy-start | bytes 5087236
  13.5 51.8 %collective-permute-start.2 = (bf16[2,18,69,256]{3,0,2,1:T(2,128)(2,1)}, bf16[2,18,69,256]{3,0,2,1:T(2,128)(2,1)}, u32[]{:S(2)}, u32[]{:S(2)}) collective-permute-start(bf16[2,18,69,256]{3,0,2,1:T(2,128)(2,1)} %copy.46), channel_id=1, source_target_pairs={{0,2},{1,3},{2,0},{3,1},{4,6},{5,7},{6,4},{7,5},{8,10},{9,11},{10,... | collective-permute-start | bytes 3815432 | tf_op jit(solution)/shard_map/ppermute | solution.py:167
  17.2 20.7 %copy-start.22 = (s32[2]{0:T(128)S(1)}, s32[2]{0:T(128)}, u32[]{:S(2)}) copy-start(s32[2]{0:T(128)} %param.13) | copy-start | bytes 28
  17.2 21.4 %copy-start.1 = (bf16[2,69,24,256]{3,1,2,0:T(8,128)(2,1)S(1)}, bf16[2,69,24,256]{3,1,2,0:T(8,128)(2,1)}, u32[]{:S(2)}) copy-start(bf16[2,69,24,256]{3,1,2,0:T(8,128)(2,1)} %copy-done) | copy-start | bytes 5087236
  34.9 22.6 %collective-permute-start.5 = (f32[2]{0:T(128)S(1)}, f32[2]{0:T(128)S(1)}, u32[]{:S(2)}, u32[]{:S(2)}) collective-permute-start(f32[2]{0:T(128)S(1)} %get-tuple-element.25), channel_id=1, source_target_pairs={{0,1},{1,2},{2,3},{3,0},{4,5},{5,6},{6,7},{7,4},{8,9},{9,10},{10,1... | collective-permute-start | bytes 32 | tf_op jit(solution)/shard_map/ppermute | solution.py:220
  34.9 24.4 %collective-permute-start.6 = (f32[2]{0:T(128)S(1)}, f32[2]{0:T(128)}, u32[]{:S(2)}, u32[]{:S(2)}) collective-permute-start(f32[2]{0:T(128)S(1)} %get-tuple-element.25), channel_id=1, source_target_pairs={{0,2},{1,3},{2,0},{3,1},{4,6},{5,7},{6,4},{7,5},{8,10},{9,11},{10,... | collective-permute-start | bytes 32 | tf_op jit(solution)/shard_map/ppermute | solution.py:220
  36.4 24.8 %collective-permute-start.7 = (f32[2]{0:T(128)S(1)}, f32[2]{0:T(128)}, u32[]{:S(2)}, u32[]{:S(2)}) collective-permute-start(f32[2]{0:T(128)S(1)} %get-tuple-element.25), channel_id=1, source_target_pairs={{0,3},{1,0},{2,1},{3,2},{4,7},{5,4},{6,5},{7,6},{8,11},{9,8},{10,9... | collective-permute-start | bytes 32 | tf_op jit(solution)/shard_map/ppermute | solution.py:220
  37.9 10.9 %collective-permute-start = (s32[2]{0:T(128)S(1)}, s32[2]{0:T(128)S(1)}, u32[]{:S(2)}, u32[]{:S(2)}) collective-permute-start(s32[2]{0:T(128)S(1)} %copy-done.22), channel_id=1, source_target_pairs={{0,1},{1,0},{2,3},{3,2},{4,5},{5,4},{6,7},{7,6},{8,9},{9,8},{10,11... | collective-permute-start | bytes 32 | tf_op jit(solution)/shard_map/ppermute | solution.py:186
  38.5 1.2 %copy-start.3 = (bf16[69,24,256]{2,0,1:T(8,128)(2,1)S(1)}, bf16[69,24,256]{2,0,1:T(8,128)(2,1)}, u32[]{:S(2)}) copy-start(bf16[69,24,256]{2,0,1:T(8,128)(2,1)} %copy.66) | copy-start | bytes 2543620
  48.8 20.9 %collective-permute-start.1 = (bf16[2,6,69,256]{3,2,1,0:T(8,128)(2,1)S(1)}, bf16[2,6,69,256]{3,2,1,0:T(8,128)(2,1)S(1)}, u32[]{:S(2)}, u32[]{:S(2)}) collective-permute-start(bf16[2,6,69,256]{3,2,1,0:T(8,128)(2,1)S(1)} %update_chunk.3), channel_id=1, source_target_pairs={{0,2},{1,3},{2,0},{3,1},{4,6},{5,7},{6,4},{7,5},{8,10},{9,11},{10,... | collective-permute-start | bytes 1271816 | tf_op jit(solution)/shard_map/ppermute | solution.py:167
  70.7 5.0 %collective-permute-start.4 = (bf16[2,18,69,256]{3,0,2,1:T(2,128)(2,1)S(1)}, bf16[2,18,69,256]{3,0,2,1:T(2,128)(2,1)S(1)}, u32[]{:S(2)}, u32[]{:S(2)}) collective-permute-start(bf16[2,18,69,256]{3,0,2,1:T(2,128)(2,1)S(1)} %copy.49), channel_id=1, source_target_pairs={{0,1},{1,0},{2,3},{3,2},{4,5},{5,4},{6,7},{7,6},{8,9},{9,8},{10,11... | collective-permute-start | bytes 3815432 | tf_op jit(solution)/shard_map/ppermute | solution.py:241
  71.7 2.7 %collective-permute-start.3 = (bf16[2,6,69,256]{3,2,1,0:T(8,128)(2,1)S(1)}, bf16[2,6,69,256]{3,2,1,0:T(8,128)(2,1)S(1)}, u32[]{:S(2)}, u32[]{:S(2)}) collective-permute-start(bf16[2,6,69,256]{3,2,1,0:T(8,128)(2,1)S(1)} %pad_maximum_fusion.1), channel_id=1, source_target_pairs={{0,1},{1,0},{2,3},{3,2},{4,5},{5,4},{6,7},{7,6},{8,9},{9,8},{10,11... | collective-permute-start | bytes 1271816 | tf_op jit(solution)/shard_map/ppermute | solution.py:241
  (7 other events, 6.5 us)

commit v4 on v3

--- a/solution.py
+++ b/solution.py
@@ -94,7 +94,7 @@
             pltpu.VMEM((len(spans), (widest + 4) * hid, lat), jnp.bfloat16),
             pltpu.VMEM((len(spans), (widest + 2) * hid, lat), jnp.bfloat16),
         ],
-        compiler_params=pltpu.CompilerParams(vmem_limit_bytes=24 << 20),
+        compiler_params=pltpu.CompilerParams(vmem_limit_bytes=56 << 20),
         cost_estimate=pl.CostEstimate(flops=0, bytes_accessed=1024, transcendentals=0),
         name="update_chunk",
     )(*edges, mid, observed, obs_weight, w1, w2, w3)
@@ -168,12 +168,72 @@
     ]
 
 
-def pick(pieces, c):
-    slots = pieces[0].shape[0]
-    value = pieces[0][0]
-    for m in range(1, len(pieces) * slots):
-        value = jnp.where(c == m, pieces[m // slots][m % slots], value)
-    return value
+def pick_kernel(slots, base, codes_ref, *refs):
+    *pieces, out_ref = refs
+    if base == 0:
+        received_ref, *pieces = pieces
+    for s in range(slots):
+        for m in range(len(pieces) * slots):
+            wanted = codes_ref[base + s] == m
+            if base == 0:
+                wanted = wanted & (codes_ref[2 * slots + s] == 1)
+
+            @pl.when(wanted)
+            def _():
+                out_ref[s] = pieces[m // slots][m % slots]
+
+        if base == 0:
+
+            @pl.when(codes_ref[2 * slots + s] == 0)
+            def _():
+                out_ref[s] = received_ref[s]
+
+
+def pick(codes, base, arrays):
+    u = arrays[0]
+    slots = u.shape[0]
+    vmem = pl.BlockSpec(memory_space=pltpu.VMEM)
+    return pl.pallas_call(
+        functools.partial(pick_kernel, slots, base),
+        out_shape=jax.ShapeDtypeStruct(u.shape, u.dtype),
+        in_specs=[pl.BlockSpec(memory_space=pltpu.SMEM)] + [vmem] * len(arrays),
+        out_specs=vmem,
+        compiler_params=pltpu.CompilerParams(vmem_limit_bytes=24 << 20),
+        cost_estimate=pl.CostEstimate(flops=0, bytes_accessed=1024, transcendentals=0),
+        name="pick",
+    )(codes, *arrays)
+
+
+def weight_kernel(slots, t_ref, *refs):
+    *part_refs, out_ref = refs
+    shape = out_ref.shape
+    real = lax.broadcasted_iota(jnp.int32, shape, 0) < slots
+    count = len(part_refs) * slots
+
+    def over_particles(rows):
+        total = rows[0]
+        for row in rows[1:]:
+            total = total + row
+        return jnp.sum(total, axis=0, keepdims=True)
+
+    misfits = [jnp.broadcast_to(jnp.sum(r[...], axis=1, keepdims=True), shape) for r in part_refs]
+    center = over_particles([jnp.where(real, m, 0.0) for m in misfits]) / count
+    deviations = [jnp.where(real, m - center, 0.0) for m in misfits]
+    spread = jnp.sqrt(over_particles([d * d for d in deviations]) / count + 1.0)
+    expos = [jnp.where(real, jnp.exp(-0.5 * t_ref[0] * d / spread), 0.0) for d in deviations]
+    out_ref[...] = expos[0] / over_particles(expos)
+
+
+def own_weights_of(parts, tempering, slots):
+    vmem = pl.BlockSpec(memory_space=pltpu.VMEM)
+    out = pl.pallas_call(
+        functools.partial(weight_kernel, slots),
+        out_shape=jax.ShapeDtypeStruct(parts[0].shape, jnp.float32),
+        in_specs=[pl.BlockSpec(memory_space=pltpu.SMEM)] + [vmem] * len(parts),
+        out_specs=vmem,
+        name="own_weights",
+    )(tempering, *parts)
+    return out[:slots, 0]
 
 
 def on_device(particles, observed, precision, stations, ancestors, tempering, w_in, w_mid, w_out):
@@ -213,35 +273,22 @@
     low, high, band_sums = exchange(mid, sums, n_lon)
     groups.append(across(update([(0, 3), (cols - 3, cols)], [low, high])))
 
-    own_misfit = jnp.sum(band_sums[:slots], axis=1)
-    every_sum = jnp.concatenate(
-        [own_misfit]
-        + [
-            lax.ppermute(own_misfit, "dom", [(d, (d + k) % n_dom) for d in range(n_dom)])
-            for k in range(1, n_dom)
-        ]
-    )
-    center = jnp.mean(every_sum)
-    deviation = every_sum - center
-    spread = jnp.sqrt(jnp.mean(deviation * deviation) + 1.0)
-    expo = jnp.exp(-0.5 * tempering[0] * deviation / spread)
-    own_weights = expo[:slots] / jnp.sum(expo)
-
-    done, before = [], None
+    parts = [band_sums] + [
+        lax.ppermute(band_sums, "dom", [(d, (d + k) % n_dom) for d in range(n_dom)])
+        for k in range(1, n_dom)
+    ]
+    own_weights = own_weights_of(parts, tempering, slots)
+
+    codes = jnp.concatenate([candidate, here[:slots].astype(jnp.int32)])
+    codes, _ = lax.optimization_barrier((codes, groups[-1][0]))
+    results, before = [], None
     for pieces in groups:
         if before is not None:
             *pieces, before = lax.optimization_barrier((*pieces, before))
-            done[-1] = before
-        sent = jnp.stack([pick(pieces, candidate[slots + s]) for s in range(slots)])
+        sent = pick(codes, slots, pieces)
         before = sent
-        done.append(sent)
-        groups[len(done) - 1] = pieces
-    results = []
-    for pieces, sent in zip(groups, done):
         received = lax.ppermute(sent, "dom", [(d, d ^ 1) for d in range(n_dom)])
-        results.append(
-            jnp.stack([jnp.where(here[s], pick(pieces, candidate[s]), received[s]) for s in range(slots)])
-        )
+        results.append(pick(codes, 0, [received, *pieces]))
     inner, sides = results
     new_columns = jnp.concatenate([sides[:, :3], inner, sides[:, 3:]], axis=1)
     return (new_columns.transpose(0, 2, 1, 3), own_weights)

time: 81.5 us -> 81.8 us (level)
  waiting for transfers between devices: 0.5 us -> 15.3 us
  other arithmetic: 12.3 us -> 1.16 us
  Pallas kernels: 24.9 us -> 35.7 us
  between operations: 12.2 us -> 1.5 us
  local copies, waits for them, and re-layouts: 23.7 us -> 19.9 us
    ppermute x2, waiting for transfers between devices: 0.01 us -> 14.6 us  [across(): lax.ppermute(u, 'dom', [(d, (d + 2 * k) % n) for d in range(n)])]
    reduce_sum x6 -> x0, other arithmetic: 6.51 us -> none  [the longest x4 4.45 us: on_device(): center = jnp.mean(every_sum)]
    unnamed x49 -> x29, local copies, waits for them, and re-layouts: 12.2 us -> 5.94 us
    slice x4 -> x2, local copies, waits for them, and re-layouts: 6.83 us -> 1.33 us  [the longest x1 1.3 us: own_weights_of(): return out[:slots, 0]]
    pallas_call x0 -> x5, Pallas kernels: none -> 5.34 us  [the longest x4 3.91 us: pick(): pl.pallas_call(functools.partial(pick_kernel, slots, base), out_shape=jax...]
    pallas_call x2, Pallas kernels: 9.11 us -> 13.7 us  [update_chunk(): pl.pallas_call(functools.partial(step_kernel, spans, cin, hid, bool(edges...]
    select_n x5 -> x0, other arithmetic: 3.36 us -> none  [the longest x2 2.86 us: on_device(): jnp.where(here[s], pick(pieces, candidate[s]), received[s])]
    ppermute x0 -> x2, local copies, waits for them, and re-layouts: none -> 3 us  [the longest x1 1.5 us: on_device(): received = lax.ppermute(sent, 'dom', [(d, d ^ 1) for d in range(n_dom)])]
  transfers between devices with their start and end apart: 8 -> 8, of which waited for: 1 -> 4; matrix products, arithmetic and copies ran while one was open for 20% -> 4% of each run, Pallas kernels for 24% -> 33%
where the time goes in v4:
time: 81.8 us; the launch traced here: 81.3 us
  Pallas kernels  35.7 us (44%)
  local copies, waits for them, and re-layouts  19.9 us (24%)
  waiting for transfers between devices  15.3 us (19%)
  starting transfers between devices  7.89 us (10%)
  between operations  1.5 us (2%)
  other arithmetic  1.16 us (1%)
    pallas_call x1, Pallas kernels, exchange(): pl.pallas_call(functools.partial(exchange_kernel, n_lon), out_shape=(edge...  16.7 us
    ppermute x2, waiting for transfers between devices, across(): lax.ppermute(u, 'dom', [(d, (d + 2 * k) % n) for d in range(n)])  14.6 us
    pallas_call x2, Pallas kernels, update_chunk(): pl.pallas_call(functools.partial(step_kernel, spans, cin, hid, bool(edges...  13.7 us
    unnamed x29, local copies, waits for them, and re-layouts  5.94 us
    ppermute x2, starting transfers between devices, across(): lax.ppermute(u, 'dom', [(d, (d + 2 * k) % n) for d in range(n)])  4.68 us
    pallas_call x4, Pallas kernels, pick(): pl.pallas_call(functools.partial(pick_kernel, slots, base), out_shape=jax...  3.91 us
    pallas_call x1, local copies, waits for them, and re-layouts, update_chunk(): pl.pallas_call(functools.partial(step_kernel, spans, cin, hid, bool(edges...  3.38 us
    ppermute x3, starting transfers between devices, on_device(): lax.ppermute(band_sums, 'dom', [(d, (d + k) % n_dom) for d in range(n_dom)])  3.21 us
  transfers between devices with their start and end apart: 8, of which 4 were waited for; matrix products, arithmetic and copies ran while one was open for 4% of the time, Pallas kernels for 33%

profile of v4, /device:TPU:0, one launch (start us, length us, event | category | flops | bytes accessed | tf_op | source)
XLA Modules:
  0.0 81.3 jit_solution(6580703387869952214)
XLA Ops:
  0.6 3.1 %copy.55 = bf16[2,69,24,256]{3,1,2,0:T(8,128)(2,1)} copy(bf16[2,69,24,256]{3,2,1,0:T(8,128)(2,1)} %param.9) | data formatting | bytes 3391488 | tf_op args[0]
  3.8 1.1 %copy.56 = bf16[69,24,256]{2,0,1:T(8,128)(2,1)} copy(bf16[69,24,256]{2,1,0:T(8,128)(2,1)S(1)} %copy-done.3) | data formatting | bytes 1695744 | tf_op args[1]
  5.7 0.8 reshape.18.refs_3_.refs_5_
  6.6 0.8 reshape.19.refs_4_.refs_6_
  7.7 0.8 %reshape.22.refs_5_.refs_7_ = bf16[240,192]{1,0:T(8,128)(2,1)} reshape(bf16[3,80,3,64]{3,2,1,0:T(4,128)(2,1)S(1)} %copy.51) | data formatting | bytes 184320 | tf_op jit(solution)/shard_map/reshape | solution.py:18
  8.5 7.4 %update_chunk.2.refs_0_.refs_1_ = bf16[2,18,69,256]{3,2,1,0:T(8,128)(2,1)} custom-call(bf16[2,24,69,256]{3,2,1,0:T(8,128)(2,1)} %bitcast.13, bf16[24,69,256]{2,1,0:T(8,128)(2,1)} %bitcast.16, f32[24,1,256]{2,1,0:T(1,128)} %broadcast_in_dim.2.refs_2_.refs_4_, bf16[192,240]{1,0:T(8,128)(2,1)} %reshape.18.refs_3_.refs_5_, ...), custom_call_target="tpu_custom_call" | custom-call | bytes 1024 | tf_op jit(solution)/shard_map/update_chunk/pallas_call | solution.py:85
  15.9 3.4 %copy.45 = bf16[2,18,69,256]{3,0,2,1:T(2,128)(2,1)} copy(bf16[2,18,69,256]{3,2,1,0:T(8,128)(2,1)} %update_chunk.2.refs_0_.refs_1_) | data formatting | bytes 2543616 | tf_op jit(solution)/shard_map/update_chunk/pallas_call | solution.py:85
  19.3 2.9 %collective-permute-start.2 = (bf16[2,18,69,256]{3,0,2,1:T(2,128)(2,1)}, bf16[2,18,69,256]{3,0,2,1:T(2,128)(2,1)}, u32[]{:S(2)}, u32[]{:S(2)}) collective-permute-start(bf16[2,18,69,256]{3,0,2,1:T(2,128)(2,1)} %copy.45), channel_id=1, source_target_pairs={{0,2},{1,3},{2,0},{3,1},{4,6},{5,7},{6,4},{7,5},{8,10},{9,11},{10,... | collective-permute-start | bytes 3815432 | tf_op jit(solution)/shard_map/ppermute | solution.py:167
  23.6 16.7 %exchange.1 = (bf16[2,3,69,256]{3,2,1,0:T(8,128)(2,1)}, bf16[2,3,69,256]{3,2,1,0:T(8,128)(2,1)}, f32[8,128]{1,0:T(8,128)}) custom-call(bf16[2,24,69,256]{3,2,1,0:T(8,128)(2,1)} %bitcast.14, f32[8,128]{1,0:T(8,128)} %pad.14.sums_ref), custom_call_target="tpu_custom_call" | custom-call | bytes 1024 | tf_op jit(solution)/shard_map/exchange/pallas_call | solution.py:146
  40.3 6.2 %update_chunk.3.refs_0_.refs_1_ = bf16[2,6,69,256]{3,2,1,0:T(8,128)(2,1)} custom-call(bf16[2,3,69,256]{3,2,1,0:T(8,128)(2,1)} %get-tuple-element.10.refs_0_, bf16[2,3,69,256]{3,2,1,0:T(8,128)(2,1)} %get-tuple-element.11.refs_1_, bf16[2,24,69,256]{3,2,1,0:T(8,128)(2,1)} %bitcast.15, bf16[24,69,256]{2,1,0:T(8,128)(2,1)} %bitcast.17, ...), custom_call_target="tpu_custom_call" | custom-call | bytes 1024 | tf_op jit(solution)/shard_map/update_chunk/pallas_call | solution.py:85
  46.7 3.7 %collective-permute-done.2 = bf16[2,18,69,256]{3,0,2,1:T(2,128)(2,1)} collective-permute-done((bf16[2,18,69,256]{3,0,2,1:T(2,128)(2,1)}, bf16[2,18,69,256]{3,0,2,1:T(2,128)(2,1)}, u32[]{:S(2)}, u32[]{:S(2)}) %collective-permute-start.2) | collective-permute-done | bytes 1271840 | tf_op jit(solution)/shard_map/ppermute | solution.py:167
  50.5 1.5 %copy.46.refs_1_.refs_2_ = bf16[2,18,69,256]{3,2,1,0:T(8,128)(2,1)S(1)} copy(bf16[2,18,69,256]{3,0,2,1:T(2,128)(2,1)} %collective-permute-done.2) | data formatting | bytes 2543616 | tf_op jit(solution)/shard_map/ppermute | solution.py:167
  52.7 2.0 %copy.47 = bf16[2,18,69,256]{3,0,2,1:T(2,128)(2,1)} copy(bf16[2,18,69,256]{3,2,1,0:T(8,128)(2,1)S(1)} %pick.4) | data formatting | bytes 2543616 | tf_op jit(solution)/shard_map/pick/pallas_call | solution.py:196
  54.8 1.7 %collective-permute-start.1 = (bf16[2,6,69,256]{3,2,1,0:T(8,128)(2,1)S(1)}, bf16[2,6,69,256]{3,2,1,0:T(8,128)(2,1)S(1)}, u32[]{:S(2)}, u32[]{:S(2)}) collective-permute-start(bf16[2,6,69,256]{3,2,1,0:T(8,128)(2,1)S(1)} %copy-done.1), channel_id=1, source_target_pairs={{0,2},{1,3},{2,0},{3,1},{4,6},{5,7},{6,4},{7,5},{8,10},{9,11},{10,... | collective-permute-start | bytes 1271816 | tf_op jit(solution)/shard_map/ppermute | solution.py:167
  56.5 10.8 %collective-permute-done.1.refs_1_.refs_2_ = bf16[2,6,69,256]{3,2,1,0:T(8,128)(2,1)S(1)} collective-permute-done((bf16[2,6,69,256]{3,2,1,0:T(8,128)(2,1)S(1)}, bf16[2,6,69,256]{3,2,1,0:T(8,128)(2,1)S(1)}, u32[]{:S(2)}, u32[]{:S(2)}) %collective-permute-start.1) | collective-permute-done | bytes 423968 | tf_op jit(solution)/shard_map/ppermute | solution.py:167
  67.3 1.4 %pick.5 = bf16[2,6,69,256]{3,2,1,0:T(8,128)(2,1)} custom-call(s32[6]{0:T(128)S(1)} %pad_add_fusion.1.codes_ref, bf16[2,6,69,256]{3,2,1,0:T(8,128)(2,1)S(1)} %copy-done.1, bf16[2,6,69,256]{3,2,1,0:T(8,128)(2,1)S(1)} %collective-permute-done.1.refs_1_.refs_2_), custom_call_target="tpu_custom_call" | custom-call | bytes 1024 | tf_op jit(solution)/shard_map/pick/pallas_call | solution.py:196
  69.2 1.7 %collective-permute-start.6 = (f32[8,128]{1,0:T(8,128)S(1)}, f32[8,128]{1,0:T(8,128)S(1)}, u32[]{:S(2)}, u32[]{:S(2)}) collective-permute-start(f32[8,128]{1,0:T(8,128)S(1)} %copy-done.9), channel_id=1, source_target_pairs={{0,2},{1,3},{2,0},{3,1},{4,6},{5,7},{6,4},{7,5},{8,10},{9,11},{10,... | collective-permute-start | bytes 12296 | tf_op jit(solution)/shard_map/ppermute | solution.py:277
  71.0 1.0 %collective-permute-start.7 = (f32[8,128]{1,0:T(8,128)S(1)}, f32[8,128]{1,0:T(8,128)}, u32[]{:S(2)}, u32[]{:S(2)}) collective-permute-start(f32[8,128]{1,0:T(8,128)S(1)} %copy-done.9), channel_id=1, source_target_pairs={{0,3},{1,0},{2,1},{3,2},{4,7},{5,4},{6,5},{7,6},{8,11},{9,8},{10,9... | collective-permute-start | bytes 12296 | tf_op jit(solution)/shard_map/ppermute | solution.py:277
  73.4 1.4 %own_weights.1 = f32[8,128]{1,0:T(8,128)} custom-call(f32[1]{0:T(128)S(6)} %copy.57.t_ref, f32[8,128]{1,0:T(8,128)} %get-tuple-element.15.refs_0_, f32[8,128]{1,0:T(8,128)} %copy-done.10, f32[8,128]{1,0:T(8,128)} %copy-done.11, f32[8,128]{1,0:T(8,128)} %collective-permute-done.7.refs_3_), custom_call_target="tpu_custom_call" | custom-call | tf_op jit(solution)/shard_map/own_weights/pallas_call | solution.py:229
  74.9 1.3 %slice_reduce_fusion = f32[2]{0:T(128)} fusion(f32[8,128]{1,0:T(8,128)} %own_weights.1), kind=kLoop, calls=%fused_computation.17 | loop fusion | bytes 16 | tf_op jit(solution)/shard_map/slice | solution.py:236
  76.2 1.1 %pick.6 = bf16[2,6,69,256]{3,2,1,0:T(8,128)(2,1)S(1)} custom-call(s32[6]{0:T(128)S(1)} %pad_add_fusion.1.codes_ref, bf16[2,6,69,256]{3,2,1,0:T(8,128)(2,1)} %collective-permute-done.3.refs_0_, bf16[2,6,69,256]{3,2,1,0:T(8,128)(2,1)S(1)} %copy-done.1, bf16[2,6,69,256]{3,2,1,0:T(8,128)(2,1)S(1)} %collective-permute-done.1.refs_1_.refs_2_), custom_call_target="tpu_custom_call" | custom-call | bytes 1024 | tf_op jit(solution)/shard_map/pick/pallas_call | solution.py:196
  77.4 1.5 %copy.48.refs_0_ = bf16[2,18,69,256]{3,2,1,0:T(8,128)(2,1)S(1)} copy(bf16[2,18,69,256]{3,0,2,1:T(2,128)(2,1)} %collective-permute-done.4) | data formatting | bytes 2543616 | tf_op jit(solution)/shard_map/ppermute | solution.py:290
  78.9 0.7 pick.7
  79.8 1.5 %copy.50 = bf16[2,69,24,256]{3,2,1,0:T(8,128)(2,1)} copy(bf16[2,69,24,256]{3,1,2,0:T(8,128)(2,1)S(1)} %maximum_bitcast_fusion) | data formatting | bytes 3391488
  (55 shorter events, 5.0 us)
Async XLA Ops:
  0.6 3.1 %copy-start.3 = (bf16[69,24,256]{2,1,0:T(8,128)(2,1)S(1)}, bf16[69,24,256]{2,1,0:T(8,128)(2,1)}, u32[]{:S(2)}) copy-start(bf16[69,24,256]{2,1,0:T(8,128)(2,1)} %param.10) | copy-start | bytes 2543620
  3.8 1.1 %copy-start.7 = (f32[24,256]{1,0:T(8,128)S(1)}, f32[24,256]{1,0:T(8,128)}, u32[]{:S(2)}) copy-start(f32[24,256]{1,0:T(8,128)} %param.11) | copy-start | bytes 73732
  3.8 1.1 %copy-start.8 = (s32[24,256]{1,0:T(8,128)S(1)}, s32[24,256]{1,0:T(8,128)}, u32[]{:S(2)}) copy-start(s32[24,256]{1,0:T(8,128)} %param.12) | copy-start | bytes 73732
  3.8 1.8 %copy-start.4 = (bf16[3,3,64,69]{3,2,1,0:T(8,128)(2,1)S(1)}, bf16[3,3,64,69]{3,2,1,0:T(8,128)(2,1)}, u32[]{:S(2)}) copy-start(bf16[3,3,64,69]{3,2,1,0:T(8,128)(2,1)} %param.15) | copy-start | bytes 238468
  3.8 2.7 %copy-start.6 = (bf16[3,3,64,64]{3,2,1,0:T(8,128)(2,1)S(1)}, bf16[3,3,64,64]{3,2,1,0:T(8,128)(2,1)}, u32[]{:S(2)}) copy-start(bf16[3,3,64,64]{3,2,1,0:T(8,128)(2,1)} %param.16) | copy-start | bytes 221188
  3.8 3.6 %copy-start.5 = (bf16[3,3,69,64]{2,3,1,0:T(8,128)(2,1)S(1)}, bf16[3,3,69,64]{2,3,1,0:T(8,128)(2,1)}, u32[]{:S(2)}) copy-start(bf16[3,3,69,64]{2,3,1,0:T(8,128)(2,1)} %param.17) | copy-start | bytes 238468
  15.9 6.3 %copy-start.12 = (s32[2]{0:T(128)S(1)}, s32[2]{0:T(128)}, u32[]{:S(2)}) copy-start(s32[2]{0:T(128)} %param.13) | copy-start | bytes 28
  19.3 3.1 %copy-start.2 = (bf16[2,69,24,256]{3,2,1,0:T(8,128)(2,1)S(1)}, bf16[2,69,24,256]{3,2,1,0:T(8,128)(2,1)}, u32[]{:S(2)}) copy-start(bf16[2,69,24,256]{3,2,1,0:T(8,128)(2,1)} %param.9) | copy-start | bytes 5087236
  19.3 31.2 %collective-permute-start.2 = (bf16[2,18,69,256]{3,0,2,1:T(2,128)(2,1)}, bf16[2,18,69,256]{3,0,2,1:T(2,128)(2,1)}, u32[]{:S(2)}, u32[]{:S(2)}) collective-permute-start(bf16[2,18,69,256]{3,0,2,1:T(2,128)(2,1)} %copy.45), channel_id=1, source_target_pairs={{0,2},{1,3},{2,0},{3,1},{4,6},{5,7},{6,4},{7,5},{8,10},{9,11},{10,... | collective-permute-start | bytes 3815432 | tf_op jit(solution)/shard_map/ppermute | solution.py:167
  22.3 24.3 %collective-permute-start = (s32[2]{0:T(128)S(1)}, s32[2]{0:T(128)S(1)}, u32[]{:S(2)}, u32[]{:S(2)}) collective-permute-start(s32[2]{0:T(128)S(1)} %copy-done.12), channel_id=1, source_target_pairs={{0,1},{1,0},{2,3},{3,2},{4,5},{5,4},{6,7},{7,6},{8,9},{9,8},{10,11... | collective-permute-start | bytes 32 | tf_op jit(solution)/shard_map/ppermute | solution.py:246
  46.5 5.5 %copy-start = (bf16[2,18,69,256]{3,2,1,0:T(8,128)(2,1)S(1)}, bf16[2,18,69,256]{3,2,1,0:T(8,128)(2,1)}, u32[]{:S(2)}) copy-start(bf16[2,18,69,256]{3,2,1,0:T(8,128)(2,1)} %update_chunk.2.refs_0_.refs_1_) | copy-start | bytes 3815428
  52.7 2.1 %copy-start.1 = (bf16[2,6,69,256]{3,2,1,0:T(8,128)(2,1)S(1)}, bf16[2,6,69,256]{3,2,1,0:T(8,128)(2,1)}, u32[]{:S(2)}) copy-start(bf16[2,6,69,256]{3,2,1,0:T(8,128)(2,1)} %update_chunk.3.refs_0_.refs_1_) | copy-start | bytes 1271812
  52.7 16.0 %copy-start.9 = (f32[8,128]{1,0:T(8,128)S(1)}, f32[8,128]{1,0:T(8,128)}, u32[]{:S(2)}) copy-start(f32[8,128]{1,0:T(8,128)} %get-tuple-element.15.refs_0_) | copy-start | bytes 12292
  54.8 22.6 %collective-permute-start.4 = (bf16[2,18,69,256]{3,0,2,1:T(2,128)(2,1)}, bf16[2,18,69,256]{3,0,2,1:T(2,128)(2,1)}, u32[]{:S(2)}, u32[]{:S(2)}) collective-permute-start(bf16[2,18,69,256]{3,0,2,1:T(2,128)(2,1)} %copy.47), channel_id=1, source_target_pairs={{0,1},{1,0},{2,3},{3,2},{4,5},{5,4},{6,7},{7,6},{8,9},{9,8},{10,11... | collective-permute-start | bytes 3815432 | tf_op jit(solution)/shard_map/ppermute | solution.py:290
  54.8 12.6 %collective-permute-start.1 = (bf16[2,6,69,256]{3,2,1,0:T(8,128)(2,1)S(1)}, bf16[2,6,69,256]{3,2,1,0:T(8,128)(2,1)S(1)}, u32[]{:S(2)}, u32[]{:S(2)}) collective-permute-start(bf16[2,6,69,256]{3,2,1,0:T(8,128)(2,1)S(1)} %copy-done.1), channel_id=1, source_target_pairs={{0,2},{1,3},{2,0},{3,1},{4,6},{5,7},{6,4},{7,5},{8,10},{9,11},{10,... | collective-permute-start | bytes 1271816 | tf_op jit(solution)/shard_map/ppermute | solution.py:167
  68.7 7.4 %collective-permute-start.3 = (bf16[2,6,69,256]{3,2,1,0:T(8,128)(2,1)}, bf16[2,6,69,256]{3,2,1,0:T(8,128)(2,1)}, u32[]{:S(2)}, u32[]{:S(2)}) collective-permute-start(bf16[2,6,69,256]{3,2,1,0:T(8,128)(2,1)} %pick.5), channel_id=1, source_target_pairs={{0,1},{1,0},{2,3},{3,2},{4,5},{5,4},{6,7},{7,6},{8,9},{9,8},{10,11... | collective-permute-start | bytes 1271816 | tf_op jit(solution)/shard_map/ppermute | solution.py:290
  68.7 3.9 %collective-permute-start.5 = (f32[8,128]{1,0:T(8,128)S(1)}, f32[8,128]{1,0:T(8,128)S(1)}, u32[]{:S(2)}, u32[]{:S(2)}) collective-permute-start(f32[8,128]{1,0:T(8,128)S(1)} %copy-done.9), channel_id=1, source_target_pairs={{0,1},{1,2},{2,3},{3,0},{4,5},{5,6},{6,7},{7,4},{8,9},{9,10},{10,1... | collective-permute-start | bytes 12296 | tf_op jit(solution)/shard_map/ppermute | solution.py:277
  69.2 3.6 %collective-permute-start.6 = (f32[8,128]{1,0:T(8,128)S(1)}, f32[8,128]{1,0:T(8,128)S(1)}, u32[]{:S(2)}, u32[]{:S(2)}) collective-permute-start(f32[8,128]{1,0:T(8,128)S(1)} %copy-done.9), channel_id=1, source_target_pairs={{0,2},{1,3},{2,0},{3,1},{4,6},{5,7},{6,4},{7,5},{8,10},{9,11},{10,... | collective-permute-start | bytes 12296 | tf_op jit(solution)/shard_map/ppermute | solution.py:277
  71.0 2.3 %collective-permute-start.7 = (f32[8,128]{1,0:T(8,128)S(1)}, f32[8,128]{1,0:T(8,128)}, u32[]{:S(2)}, u32[]{:S(2)}) collective-permute-start(f32[8,128]{1,0:T(8,128)S(1)} %copy-done.9), channel_id=1, source_target_pairs={{0,3},{1,0},{2,1},{3,2},{4,7},{5,4},{6,5},{7,6},{8,11},{9,8},{10,9... | collective-permute-start | bytes 12296 | tf_op jit(solution)/shard_map/ppermute | solution.py:277
  72.6 0.7 copy-start.10
  72.8 0.6 copy-start.11

commit v5 on v4

--- a/solution.py
+++ b/solution.py
@@ -280,13 +280,10 @@
     own_weights = own_weights_of(parts, tempering, slots)
 
     codes = jnp.concatenate([candidate, here[:slots].astype(jnp.int32)])
-    codes, _ = lax.optimization_barrier((codes, groups[-1][0]))
-    results, before = [], None
+    groups = lax.optimization_barrier(groups)
+    results = []
     for pieces in groups:
-        if before is not None:
-            *pieces, before = lax.optimization_barrier((*pieces, before))
         sent = pick(codes, slots, pieces)
-        before = sent
         received = lax.ppermute(sent, "dom", [(d, d ^ 1) for d in range(n_dom)])
         results.append(pick(codes, 0, [received, *pieces]))
     inner, sides = results

time: 81.8 us -> 81.1 us (level)
  starting transfers between devices: 7.89 us -> 6.06 us
  other arithmetic: 1.16 us -> 2 us
    ppermute x2, waiting for transfers between devices: 14.6 us -> 12.5 us  [across(): lax.ppermute(u, 'dom', [(d, (d + 2 * k) % n) for d in range(n)])]
    transpose x4, local copies, waits for them, and re-layouts: 0.32 us -> 2.27 us  [stacked_taps(): return w.transpose(1, 2, 0, 3).reshape(3 * out_rows, 3 * in_rows)]
    ppermute x3, waiting for transfers between devices: 0.66 us -> 2.33 us  [on_device(): lax.ppermute(band_sums, 'dom', [(d, (d + k) % n_dom) for d in range(n_dom)])]
    optimization_barrier x0 -> x1, local copies, waits for them, and re-layouts: none -> 1.5 us  [on_device(): groups = lax.optimization_barrier(groups)]
    ppermute x1 -> x0, local copies, waits for them, and re-layouts: 1.5 us -> none  [across(): lax.ppermute(u, 'dom', [(d, (d + 2 * k) % n) for d in range(n)])]
    ppermute x3, starting transfers between devices: 3.21 us -> 1.97 us  [on_device(): lax.ppermute(band_sums, 'dom', [(d, (d + k) % n_dom) for d in range(n_dom)])]
    unnamed x29 -> x23, local copies, waits for them, and re-layouts: 5.94 us -> 4.79 us
    ppermute x2, starting transfers between devices: 4.68 us -> 3.57 us  [across(): lax.ppermute(u, 'dom', [(d, (d + 2 * k) % n) for d in range(n)])]
  transfers between devices with their start and end apart: 8 -> 8, of which waited for: 4 -> 3; matrix products, arithmetic and copies ran while one was open for 4% -> 4% of each run, Pallas kernels for 33% -> 33%
where the time goes in v5:
time: 81.1 us; the launch traced here: 80.7 us
  Pallas kernels  35.7 us (44%)
  local copies, waits for them, and re-layouts  20.6 us (25%)
  waiting for transfers between devices  14.8 us (18%)
  starting transfers between devices  6.06 us (7%)
  other arithmetic  2 us (2%)
  between operations  1.47 us (2%)
    pallas_call x1, Pallas kernels, exchange(): pl.pallas_call(functools.partial(exchange_kernel, n_lon), out_shape=(edge...  16.7 us
    pallas_call x2, Pallas kernels, update_chunk(): pl.pallas_call(functools.partial(step_kernel, spans, cin, hid, bool(edges...  13.7 us
    ppermute x2, waiting for transfers between devices, across(): lax.ppermute(u, 'dom', [(d, (d + 2 * k) % n) for d in range(n)])  12.5 us
    unnamed x23, local copies, waits for them, and re-layouts  4.79 us
    pallas_call x4, Pallas kernels, pick(): pl.pallas_call(functools.partial(pick_kernel, slots, base), out_shape=jax...  3.92 us
    ppermute x2, starting transfers between devices, across(): lax.ppermute(u, 'dom', [(d, (d + 2 * k) % n) for d in range(n)])  3.57 us
    pallas_call x1, local copies, waits for them, and re-layouts, update_chunk(): pl.pallas_call(functools.partial(step_kernel, spans, cin, hid, bool(edges...  3.37 us
    reshape x4, local copies, waits for them, and re-layouts, stacked_taps(): return w.transpose(1, 2, 0, 3).reshape(3 * out_rows, 3 * in_rows)  2.6 us
  transfers between devices with their start and end apart: 8, of which 3 were waited for; matrix products, arithmetic and copies ran while one was open for 4% of the time, Pallas kernels for 33%

profile of v5, /device:TPU:0, one launch (start us, length us, event | category | flops | bytes accessed | tf_op | source)
XLA Modules:
  0.0 80.7 jit_solution(2858500158212288743)
XLA Ops:
  0.7 0.8 %convert_multiply_fusion = f32[24,256]{1,0:T(8,128)S(1)} fusion(f32[24,256]{1,0:T(8,128)} %param.11, s32[24,256]{1,0:T(8,128)} %param.12), kind=kLoop, calls=%fused_computation.7 | loop fusion | flops 12288 | bytes 73728 | tf_op jit(solution)/shard_map/mul | solution.py:248
  2.1 0.9 %pad_bitcast_fusion.1 = bf16[3,64,3,80]{3,1,0,2:T(8,128)(2,1)S(1)} fusion(bf16[3,3,64,69]{3,2,1,0:T(8,128)(2,1)} %param.15), kind=kLoop, calls=%fused_computation.6 | loop fusion | bytes 171648 | tf_op jit(solution)/shard_map/transpose | solution.py:18
  3.2 0.8 reshape.18.refs_3_.refs_5_
  4.0 1.1 %pad_bitcast_fusion = bf16[3,80,3,64]{1,3,0,2:T(8,128)(2,1)S(1)} fusion(bf16[3,3,69,64]{2,3,1,0:T(8,128)(2,1)} %param.17), kind=kLoop, calls=%fused_computation.5 | loop fusion | bytes 171648 | tf_op jit(solution)/shard_map/transpose | solution.py:18
  5.2 0.8 %reshape.22.refs_5_.refs_7_ = bf16[240,192]{1,0:T(8,128)(2,1)} reshape(bf16[3,80,3,64]{3,2,1,0:T(4,128)(2,1)S(1)} %copy.51) | data formatting | bytes 184320 | tf_op jit(solution)/shard_map/reshape | solution.py:18
  6.2 0.8 reshape.19.refs_4_.refs_6_
  7.0 1.1 %copy.56 = bf16[69,24,256]{2,0,1:T(8,128)(2,1)} copy(bf16[69,24,256]{2,1,0:T(8,128)(2,1)S(1)} %copy-done.4) | data formatting | bytes 1695744 | tf_op args[1]
  8.1 1.6 %copy.55 = bf16[2,69,24,256]{3,1,2,0:T(8,128)(2,1)} copy(bf16[2,69,24,256]{3,2,1,0:T(8,128)(2,1)S(1)} %copy-done.2) | data formatting | bytes 3391488 | tf_op args[0]
  9.7 7.4 %update_chunk.2.refs_0_.refs_1_ = bf16[2,18,69,256]{3,2,1,0:T(8,128)(2,1)} custom-call(bf16[2,24,69,256]{3,2,1,0:T(8,128)(2,1)} %bitcast.13, bf16[24,69,256]{2,1,0:T(8,128)(2,1)} %bitcast.16, f32[24,1,256]{2,1,0:T(1,128)} %broadcast_in_dim.2.refs_2_.refs_4_, bf16[192,240]{1,0:T(8,128)(2,1)} %reshape.18.refs_3_.refs_5_, ...), custom_call_target="tpu_custom_call" | custom-call | bytes 1024 | tf_op jit(solution)/shard_map/update_chunk/pallas_call | solution.py:85
  17.1 3.4 %copy.44 = bf16[2,18,69,256]{3,0,2,1:T(2,128)(2,1)} copy(bf16[2,18,69,256]{3,2,1,0:T(8,128)(2,1)} %update_chunk.2.refs_0_.refs_1_) | data formatting | bytes 2543616 | tf_op jit(solution)/shard_map/update_chunk/pallas_call | solution.py:85
  20.5 2.9 %collective-permute-start.1 = (bf16[2,18,69,256]{3,0,2,1:T(2,128)(2,1)}, bf16[2,18,69,256]{3,0,2,1:T(2,128)(2,1)}, u32[]{:S(2)}, u32[]{:S(2)}) collective-permute-start(bf16[2,18,69,256]{3,0,2,1:T(2,128)(2,1)} %copy.44), channel_id=1, source_target_pairs={{0,2},{1,3},{2,0},{3,1},{4,6},{5,7},{6,4},{7,5},{8,10},{9,11},{10,... | collective-permute-start | bytes 3815432 | tf_op jit(solution)/shard_map/ppermute | solution.py:167
  24.8 16.7 %exchange.1 = (bf16[2,3,69,256]{3,2,1,0:T(8,128)(2,1)}, bf16[2,3,69,256]{3,2,1,0:T(8,128)(2,1)}, f32[8,128]{1,0:T(8,128)}) custom-call(bf16[2,24,69,256]{3,2,1,0:T(8,128)(2,1)} %bitcast.14, f32[8,128]{1,0:T(8,128)} %pad.14.sums_ref), custom_call_target="tpu_custom_call" | custom-call | bytes 1024 | tf_op jit(solution)/shard_map/exchange/pallas_call | solution.py:146
  41.5 6.2 %update_chunk.3.refs_0_.refs_1_ = bf16[2,6,69,256]{3,2,1,0:T(8,128)(2,1)} custom-call(bf16[2,3,69,256]{3,2,1,0:T(8,128)(2,1)} %get-tuple-element.11.refs_0_, bf16[2,3,69,256]{3,2,1,0:T(8,128)(2,1)} %get-tuple-element.12.refs_1_, bf16[2,24,69,256]{3,2,1,0:T(8,128)(2,1)} %bitcast.15, bf16[24,69,256]{2,1,0:T(8,128)(2,1)} %bitcast.17, ...), custom_call_target="tpu_custom_call" | custom-call | bytes 1024 | tf_op jit(solution)/shard_map/update_chunk/pallas_call | solution.py:85
  48.6 12.5 %collective-permute-done.2.refs_1_.refs_2_ = bf16[2,6,69,256]{3,2,1,0:T(8,128)(2,1)S(1)} collective-permute-done((bf16[2,6,69,256]{3,2,1,0:T(8,128)(2,1)}, bf16[2,6,69,256]{3,2,1,0:T(8,128)(2,1)S(1)}, u32[]{:S(2)}, u32[]{:S(2)}) %collective-permute-start.2) | collective-permute-done | bytes 423968 | tf_op jit(solution)/shard_map/ppermute | solution.py:167
  61.1 1.5 %copy.46.refs_1_.refs_2_ = bf16[2,18,69,256]{3,2,1,0:T(8,128)(2,1)S(1)} copy(bf16[2,18,69,256]{3,0,2,1:T(2,128)(2,1)} %collective-permute-done.1) | data formatting | bytes 2543616 | tf_op jit(solution)/shard_map/optimization_barrier | solution.py:283
  63.3 2.0 %copy.47 = bf16[2,18,69,256]{3,0,2,1:T(2,128)(2,1)} copy(bf16[2,18,69,256]{3,2,1,0:T(8,128)(2,1)S(1)} %pick.6) | data formatting | bytes 2543616 | tf_op jit(solution)/shard_map/pick/pallas_call | solution.py:196
  65.3 1.4 %pick.4 = bf16[2,6,69,256]{3,2,1,0:T(8,128)(2,1)} custom-call(s32[6]{0:T(128)S(1)} %pad_add_fusion.1.codes_ref, bf16[2,6,69,256]{3,2,1,0:T(8,128)(2,1)S(1)} %copy-done.1, bf16[2,6,69,256]{3,2,1,0:T(8,128)(2,1)S(1)} %collective-permute-done.2.refs_1_.refs_2_), custom_call_target="tpu_custom_call" | custom-call | bytes 1024 | tf_op jit(solution)/shard_map/pick/pallas_call | solution.py:196
  67.2 1.4 %collective-permute-start.7 = (f32[8,128]{1,0:T(8,128)S(1)}, f32[8,128]{1,0:T(8,128)S(1)}, u32[]{:S(2)}, u32[]{:S(2)}) collective-permute-start(f32[8,128]{1,0:T(8,128)S(1)} %copy-done.6), channel_id=1, source_target_pairs={{0,3},{1,0},{2,1},{3,2},{4,7},{5,4},{6,5},{7,6},{8,11},{9,8},{10,9... | collective-permute-start | bytes 12296 | tf_op jit(solution)/shard_map/ppermute | solution.py:277
  69.9 2.3 %collective-permute-done.6.refs_2_ = f32[8,128]{1,0:T(8,128)S(1)} collective-permute-done((f32[8,128]{1,0:T(8,128)S(1)}, f32[8,128]{1,0:T(8,128)S(1)}, u32[]{:S(2)}, u32[]{:S(2)}) %collective-permute-start.6) | collective-permute-done | bytes 4128 | tf_op jit(solution)/shard_map/ppermute | solution.py:277
  72.8 1.4 %own_weights.1 = f32[8,128]{1,0:T(8,128)} custom-call(f32[1]{0:T(128)S(6)} %copy.57.t_ref, f32[8,128]{1,0:T(8,128)} %get-tuple-element.17.refs_0_, f32[8,128]{1,0:T(8,128)} %collective-permute-done.5.refs_1_, f32[8,128]{1,0:T(8,128)} %copy-done.8, f32[8,128]{1,0:T(8,128)} %copy-done.7), custom_call_target="tpu_custom_call" | custom-call | tf_op jit(solution)/shard_map/own_weights/pallas_call | solution.py:229
  74.2 1.3 %slice_reduce_fusion = f32[2]{0:T(128)} fusion(f32[8,128]{1,0:T(8,128)} %own_weights.1), kind=kLoop, calls=%fused_computation.17 | loop fusion | bytes 16 | tf_op jit(solution)/shard_map/slice | solution.py:236
  75.5 1.1 %pick.5 = bf16[2,6,69,256]{3,2,1,0:T(8,128)(2,1)S(1)} custom-call(s32[6]{0:T(128)S(1)} %pad_add_fusion.1.codes_ref, bf16[2,6,69,256]{3,2,1,0:T(8,128)(2,1)} %collective-permute-done.3.refs_0_, bf16[2,6,69,256]{3,2,1,0:T(8,128)(2,1)S(1)} %copy-done.1, bf16[2,6,69,256]{3,2,1,0:T(8,128)(2,1)S(1)} %collective-permute-done.2.refs_1_.refs_2_), custom_call_target="tpu_custom_call" | custom-call | bytes 1024 | tf_op jit(solution)/shard_map/pick/pallas_call | solution.py:196
  76.7 1.5 %copy.48.refs_0_ = bf16[2,18,69,256]{3,2,1,0:T(8,128)(2,1)S(1)} copy(bf16[2,18,69,256]{3,0,2,1:T(2,128)(2,1)} %collective-permute-done.4) | data formatting | bytes 2543616 | tf_op jit(solution)/shard_map/ppermute | solution.py:287
  79.1 1.5 %copy.50 = bf16[2,69,24,256]{3,2,1,0:T(8,128)(2,1)} copy(bf16[2,69,24,256]{3,1,2,0:T(8,128)(2,1)S(1)} %maximum_bitcast_fusion) | data formatting | bytes 3391488
  (49 shorter events, 6.7 us)
Async XLA Ops:
  0.6 5.5 %copy-start.5 = (bf16[3,3,64,64]{3,2,1,0:T(8,128)(2,1)S(1)}, bf16[3,3,64,64]{3,2,1,0:T(8,128)(2,1)}, u32[]{:S(2)}) copy-start(bf16[3,3,64,64]{3,2,1,0:T(8,128)(2,1)} %param.16) | copy-start | bytes 221188
  0.6 6.4 %copy-start.4 = (bf16[69,24,256]{2,1,0:T(8,128)(2,1)S(1)}, bf16[69,24,256]{2,1,0:T(8,128)(2,1)}, u32[]{:S(2)}) copy-start(bf16[69,24,256]{2,1,0:T(8,128)(2,1)} %param.10) | copy-start | bytes 2543620
  4.0 4.1 %copy-start.2 = (bf16[2,69,24,256]{3,2,1,0:T(8,128)(2,1)S(1)}, bf16[2,69,24,256]{3,2,1,0:T(8,128)(2,1)}, u32[]{:S(2)}) copy-start(bf16[2,69,24,256]{3,2,1,0:T(8,128)(2,1)} %param.9) | copy-start | bytes 5087236
  17.1 6.3 %copy-start.9 = (s32[2]{0:T(128)S(1)}, s32[2]{0:T(128)}, u32[]{:S(2)}) copy-start(s32[2]{0:T(128)} %param.13) | copy-start | bytes 28
  20.5 3.1 %copy-start.3 = (bf16[2,69,24,256]{3,2,1,0:T(8,128)(2,1)S(1)}, bf16[2,69,24,256]{3,2,1,0:T(8,128)(2,1)}, u32[]{:S(2)}) copy-start(bf16[2,69,24,256]{3,2,1,0:T(8,128)(2,1)} %param.9) | copy-start | bytes 5087236
  20.5 40.6 %collective-permute-start.1 = (bf16[2,18,69,256]{3,0,2,1:T(2,128)(2,1)}, bf16[2,18,69,256]{3,0,2,1:T(2,128)(2,1)}, u32[]{:S(2)}, u32[]{:S(2)}) collective-permute-start(bf16[2,18,69,256]{3,0,2,1:T(2,128)(2,1)} %copy.44), channel_id=1, source_target_pairs={{0,2},{1,3},{2,0},{3,1},{4,6},{5,7},{6,4},{7,5},{8,10},{9,11},{10,... | collective-permute-start | bytes 3815432 | tf_op jit(solution)/shard_map/ppermute | solution.py:167
  23.4 24.9 %collective-permute-start = (s32[2]{0:T(128)S(1)}, s32[2]{0:T(128)S(1)}, u32[]{:S(2)}, u32[]{:S(2)}) collective-permute-start(s32[2]{0:T(128)S(1)} %copy-done.9), channel_id=1, source_target_pairs={{0,1},{1,0},{2,3},{3,2},{4,5},{5,4},{6,7},{7,6},{8,9},{9,8},{10,11... | collective-permute-start | bytes 32 | tf_op jit(solution)/shard_map/ppermute | solution.py:246
  47.7 14.8 %copy-start = (bf16[2,18,69,256]{3,2,1,0:T(8,128)(2,1)S(1)}, bf16[2,18,69,256]{3,2,1,0:T(8,128)(2,1)}, u32[]{:S(2)}) copy-start(bf16[2,18,69,256]{3,2,1,0:T(8,128)(2,1)} %update_chunk.2.refs_0_.refs_1_) | copy-start | bytes 3815428
  47.7 13.3 %collective-permute-start.2 = (bf16[2,6,69,256]{3,2,1,0:T(8,128)(2,1)}, bf16[2,6,69,256]{3,2,1,0:T(8,128)(2,1)S(1)}, u32[]{:S(2)}, u32[]{:S(2)}) collective-permute-start(bf16[2,6,69,256]{3,2,1,0:T(8,128)(2,1)} %update_chunk.3.refs_0_.refs_1_), channel_id=1, source_target_pairs={{0,2},{1,3},{2,0},{3,1},{4,6},{5,7},{6,4},{7,5},{8,10},{9,11},{10,... | collective-permute-start | bytes 1271816 | tf_op jit(solution)/shard_map/ppermute | solution.py:167
  63.3 2.1 %copy-start.1 = (bf16[2,6,69,256]{3,2,1,0:T(8,128)(2,1)S(1)}, bf16[2,6,69,256]{3,2,1,0:T(8,128)(2,1)}, u32[]{:S(2)}) copy-start(bf16[2,6,69,256]{3,2,1,0:T(8,128)(2,1)} %update_chunk.3.refs_0_.refs_1_) | copy-start | bytes 1271812
  63.3 3.9 %copy-start.6 = (f32[8,128]{1,0:T(8,128)S(1)}, f32[8,128]{1,0:T(8,128)}, u32[]{:S(2)}) copy-start(f32[8,128]{1,0:T(8,128)} %get-tuple-element.17.refs_0_) | copy-start | bytes 12292
  65.3 11.4 %collective-permute-start.4 = (bf16[2,18,69,256]{3,0,2,1:T(2,128)(2,1)}, bf16[2,18,69,256]{3,0,2,1:T(2,128)(2,1)}, u32[]{:S(2)}, u32[]{:S(2)}) collective-permute-start(bf16[2,18,69,256]{3,0,2,1:T(2,128)(2,1)} %copy.47), channel_id=1, source_target_pairs={{0,1},{1,0},{2,3},{3,2},{4,5},{5,4},{6,7},{7,6},{8,9},{9,8},{10,11... | collective-permute-start | bytes 3815432 | tf_op jit(solution)/shard_map/ppermute | solution.py:287
  66.7 8.8 %collective-permute-start.3 = (bf16[2,6,69,256]{3,2,1,0:T(8,128)(2,1)}, bf16[2,6,69,256]{3,2,1,0:T(8,128)(2,1)}, u32[]{:S(2)}, u32[]{:S(2)}) collective-permute-start(bf16[2,6,69,256]{3,2,1,0:T(8,128)(2,1)} %pick.4), channel_id=1, source_target_pairs={{0,1},{1,0},{2,3},{3,2},{4,5},{5,4},{6,7},{7,6},{8,9},{9,8},{10,11... | collective-permute-start | bytes 1271816 | tf_op jit(solution)/shard_map/ppermute | solution.py:287
  67.2 2.7 %collective-permute-start.7 = (f32[8,128]{1,0:T(8,128)S(1)}, f32[8,128]{1,0:T(8,128)S(1)}, u32[]{:S(2)}, u32[]{:S(2)}) collective-permute-start(f32[8,128]{1,0:T(8,128)S(1)} %copy-done.6), channel_id=1, source_target_pairs={{0,3},{1,0},{2,1},{3,2},{4,7},{5,4},{6,5},{7,6},{8,11},{9,8},{10,9... | collective-permute-start | bytes 12296 | tf_op jit(solution)/shard_map/ppermute | solution.py:277
  68.6 3.6 %collective-permute-start.6 = (f32[8,128]{1,0:T(8,128)S(1)}, f32[8,128]{1,0:T(8,128)S(1)}, u32[]{:S(2)}, u32[]{:S(2)}) collective-permute-start(f32[8,128]{1,0:T(8,128)S(1)} %copy-done.6), channel_id=1, source_target_pairs={{0,2},{1,3},{2,0},{3,1},{4,6},{5,7},{6,4},{7,5},{8,10},{9,11},{10,... | collective-permute-start | bytes 12296 | tf_op jit(solution)/shard_map/ppermute | solution.py:277
  69.0 3.2 %collective-permute-start.5 = (f32[8,128]{1,0:T(8,128)S(1)}, f32[8,128]{1,0:T(8,128)}, u32[]{:S(2)}, u32[]{:S(2)}) collective-permute-start(f32[8,128]{1,0:T(8,128)S(1)} %copy-done.6), channel_id=1, source_target_pairs={{0,1},{1,2},{2,3},{3,0},{4,5},{5,6},{6,7},{7,4},{8,9},{9,10},{10,1... | collective-permute-start | bytes 12296 | tf_op jit(solution)/shard_map/ppermute | solution.py:277
  69.9 2.3 %copy-start.7 = (f32[8,128]{1,0:T(8,128)}, f32[8,128]{1,0:T(8,128)S(1)}, u32[]{:S(2)}) copy-start(f32[8,128]{1,0:T(8,128)S(1)} %collective-permute-done.7.refs_3_) | copy-start | bytes 12292
  72.2 0.6 copy-start.8
